TPU v7x, 32 devices: a whole 2x2x4 slice. The times are simulated.
32 devices in a mesh: sx: 8 (over z, y), sy: 4 (over x, core).
Axes of the slice: x: 2, y: 2, z: 4, core: 2. Of those that a mesh axis runs over, the one named last changes fastest.
Arguments:
- schur: bfloat16 [8, 4096, 4096], P('sx', 'sy'), as said below
- precond: bfloat16 [8, 4096, 4096], P('sx', 'sy'), as said below
- right_side: float32 [8, 32, 2048], P('sx', None, 'sy')
- matching: int32 [8, 2048], P('sx', 'sy'), may hold values from 0 to 511, as said below
Outputs:
- solution: float32 [8, 32, 2048], P('sx', None, 'sy')
- residual: float32 [8, 32, 2048], P('sx', None, 'sy')
Inputs may be any that keep to these rules, and one draw needn't show every extreme that they name: `schur`: each subdomain's matrix is symmetric positive definite. `precond`: each subdomain's matrix is symmetric positive definite. `matching`: each aligned block of 512 entries of a row is a permutation of 0 to 511.
All inputs are finite; a program needn't handle non-finite values.
Results may differ from a plain program's by a relative error of at most 0.007.
The roundings to bfloat16 on the way count: a program that leaves them out, or rounds other values in their place, can miss the bound.
Values may be sent and summed in bfloat16 or wider, within the bound.
No kernel may reach another device: no remote copies, remote signals or barrier semaphores. Data moves between devices by JAX's collectives and lax.ppermute only.
A program may use at most 64 MiB of HBM per device.

v0:
```python
import functools

import jax
import jax.numpy as jnp
from jax import lax
from jax.experimental import pallas as pl
from jax.experimental.pallas import tpu as pltpu
from jax.sharding import PartitionSpec as P


LANES = 128
BUDGET = 55 << 20
AXES = ("sx", "sy")
HIGH = lax.Precision.HIGHEST
VMEM = pl.BlockSpec(memory_space=pltpu.VMEM)


def call(body, outs, *args, places=None, scratch=(), room=0):
    room = room or (4 << 20) + sum(2 * a.size * a.dtype.itemsize for a in args if a.ndim == 3)
    return pl.pallas_call(
        body,
        out_shape=outs,
        in_specs=places or [VMEM] * len(args),
        out_specs=jax.tree.map(lambda _: VMEM, outs),
        scratch_shapes=scratch,
        cost_estimate=pl.CostEstimate(flops=1 << 24, bytes_accessed=1 << 23, transcendentals=0),
        compiler_params=pltpu.CompilerParams(vmem_limit_bytes=room),
    )(*args)


def f32(*shape):
    return jax.ShapeDtypeStruct(shape, jnp.float32)


def bf16(*shape):
    return jax.ShapeDtypeStruct(shape, jnp.bfloat16)


def passed_along(block, distance):
    devices = range(lax.axis_size("sx"))
    route = [((i - distance) % len(devices), i) for i in devices]
    return lax.ppermute(block, "sx", route)


def swapped(block, first):
    n = lax.axis_size("sx")
    route = []
    for i in range(first, n, 2):
        j = (i + 1) % n
        route += [(i, j), (j, i)]
    return lax.ppermute(block, "sx", route)


def partner(block, distance):
    return lax.ppermute(block, "sy", [(i, i ^ distance) for i in range(lax.axis_size("sy"))])


def select(value, chosen, axis):
    k = value.shape[0]
    high = value.astype(jnp.bfloat16)
    rest = value - high.astype(jnp.float32)
    mid = rest.astype(jnp.bfloat16)
    low = (rest - mid.astype(jnp.float32)).astype(jnp.bfloat16)
    pieces = jnp.concatenate([high, mid, low], axis=0)
    picked = lax.dot_general(pieces, chosen, (((1,), (axis,)), ((), ())), preferred_element_type=jnp.float32)
    return (picked[:k] + picked[k : 2 * k]) + picked[2 * k :]


def gram(first, second):
    return lax.dot_general(first, second, (((1,), (1,)), ((), ())), precision=HIGH, preferred_element_type=jnp.float32)


def combine(coeff, block):
    return lax.dot_general(coeff, block, (((0,), (0,)), ((), ())), precision=HIGH, preferred_element_type=jnp.float32)


def pack(square):
    k = square.shape[0]
    pieces = LANES // k
    rows = k // pieces
    return jnp.concatenate([square[i * rows : (i + 1) * rows] for i in range(pieces)], axis=1)


def unpack(tile, k):
    pieces = LANES // k
    return jnp.concatenate([tile[:, i * k : (i + 1) * k] for i in range(pieces)], axis=0)


def halved(square):
    return 0.5 * (square + square.T)


def places(k):
    return lax.broadcasted_iota(jnp.int32, (k, k), 0), lax.broadcasted_iota(jnp.int32, (k, k), 1)


def pack_two(upper, lower):
    k = upper.shape[0]
    line, lane = places(k)
    tile = pack(jnp.where(line <= lane, upper, lower))
    diagonal = jnp.sum(jnp.where(line == lane, lower, 0.0), axis=0, keepdims=True)
    pad = jnp.zeros((1, LANES - k), jnp.float32)
    return [tile[i : i + 1] for i in range(tile.shape[0])] + [jnp.concatenate([diagonal, pad], axis=1)]


def unpack_two(row, k):
    line, lane = places(k)
    pieces = [row[:, i : i + LANES] for i in range(0, row.shape[1], LANES)]
    square = unpack(jnp.concatenate(pieces[:-1], axis=0), k)
    turned = square.T
    upper = jnp.where(line <= lane, square, turned)
    lower = jnp.where(line > lane, square, jnp.where(line < lane, turned, jnp.broadcast_to(pieces[-1][:, :k], (k, k))))
    return upper, lower


def solved(matrix, sides):
    k = matrix.shape[0]
    table = jnp.concatenate([matrix, sides, jnp.zeros((k, LANES - 2 * k), jnp.float32)], axis=1)
    line = lax.broadcasted_iota(jnp.int32, table.shape, 0)
    for step in range(0, k, 4):
        columns = [jnp.broadcast_to(table[:, step + i : step + i + 1], table.shape) for i in range(4)]
        rows = [table[step + i : step + i + 1] for i in range(4)]
        block = [[columns[j][step + i : step + i + 1] for j in range(4)] for i in range(4)]
        (a, b), (c, d) = block[0][:2], block[1][:2]
        scale = 1.0 / (a * d - b * c)

        def upper(x, y):
            return (d * x - b * y) * scale, (a * y - c * x) * scale

        sides = [upper(block[0][j], block[1][j]) for j in (2, 3)]
        first = upper(rows[0], rows[1])
        lower = [[block[i][j] - (block[i][0] * sides[j - 2][0] + block[i][1] * sides[j - 2][1]) for j in (2, 3)] for i in (2, 3)]
        rest = [rows[i] - (block[i][0] * first[0] + block[i][1] * first[1]) for i in (2, 3)]
        scale = 1.0 / (lower[0][0] * lower[1][1] - lower[0][1] * lower[1][0])
        third = (lower[1][1] * rest[0] - lower[0][1] * rest[1]) * scale
        fourth = (lower[0][0] * rest[1] - lower[1][0] * rest[0]) * scale
        new = [first[i] - (sides[0][i] * third + sides[1][i] * fourth) for i in (0, 1)] + [third, fourth]
        table = table - (columns[0] * new[0] + columns[1] * new[1]) - (columns[2] * new[2] + columns[3] * new[3])
        for i in range(4):
            table = jnp.where(line == step + i, new[i], table)
    return table[:, k : 2 * k]


def odd():
    return lax.rem(lax.axis_index("sx"), 2) == 1


def marks(both):
    rows, face = both.shape
    want = lax.broadcasted_iota(jnp.int32, (face, face), 0).astype(jnp.float32)
    match = jnp.broadcast_to(both[rows - 1 : rows, :], (face, face))
    return jnp.where(want == match, 1.0, 0.0).astype(jnp.bfloat16)


def chosen_kernel(both, chosen):
    chosen[...] = marks(both)


def join_kernel(both, following, residual, rounded):
    k = residual.shape[0]
    face = both.shape[1]
    residual[:, :face] = both[:k, :]
    residual[:, face:] = select(following[:k, :], marks(following), 0)
    rounded[...] = residual[...].astype(jnp.bfloat16)


def near_kernel(size, own, beside, matrix, part, rest, held, sems):
    me = lax.axis_index("sy")
    rows, width = matrix.shape[0], own.shape[1]
    step = min(256, rows)
    copies = []
    for d in range(size):
        columns = pl.ds(pl.multiple_of((me ^ d) * width, width), width)
        target = held.at[d] if d < 2 else rest.at[d - 2]
        copies.append(pltpu.make_async_copy(matrix.at[:, columns], target, sems.at[d]))
        copies[-1].start()
    for d, block in enumerate((own, beside)):
        copies[d].wait()
        for n in range(0, rows, step):
            made = lax.dot_general(
                block[...], held[d, n : n + step, :], (((1,), (1,)), ((), ())), preferred_element_type=jnp.float32
            )
            part[:, n : n + step] = made if d == 0 else part[:, n : n + step] + made
    for d in range(2, size):
        copies[d].wait()


def far_kernel(far, mode, *refs):
    blocks = refs[:far]
    rest, part, weights, chosen = refs[far : far + 4]
    rows = part.shape[1]
    half = rows // 2
    step = min(256, half)
    if mode == "first":
        product, swap_even, swap_odd, tile = refs[far + 4 :]
    elif mode == "both":
        earlier, product, swap_even, swap_odd, out = refs[far + 4 :]
    elif mode == "one":
        product, swap_even, swap_odd, out = refs[far + 4 :]
    else:
        product, passed, out = refs[far + 4 :]
    for n in range(0, rows, step):
        made = part[:, n : n + step]
        for d in range(far):
            made = made + lax.dot_general(
                blocks[d][...], rest[d, n : n + step, :], (((1,), (1,)), ((), ())), preferred_element_type=jnp.float32
            )
        product[:, n : n + step] = made
    if mode == "last":
        passed[...] = product[:, half:]
    else:
        picked = select(product[:, :half], chosen[...], 0)
        right = product[:, half:]
        swap_even[...] = jnp.where(odd(), picked, right)
        swap_odd[...] = jnp.where(odd(), right, picked)
    fresh = gram(weights[...], product[...])
    if mode == "first":
        tile[...] = halved(fresh)
    elif mode == "both":
        for i, row in enumerate(pack_two(earlier[...], halved(fresh))):
            out[:, :, i * LANES : (i + 1) * LANES] = jnp.broadcast_to(row[None], (out.shape[0], 1, LANES))
    else:
        out[...] = jnp.broadcast_to(pack(fresh)[None], out.shape)


def assembled(product, got_even, got_odd, chosen):
    half = product.shape[1] // 2
    from_left = jnp.where(odd(), got_even[...], got_odd[...])
    from_right = jnp.where(odd(), got_odd[...], got_even[...])
    left = product[:, :half] + select(from_left, chosen[...], 1)
    return jnp.concatenate([left, product[:, half:] + from_right], axis=1)


def direction_kernel(product, got_even, got_odd, chosen, search, rounded):
    search[...] = assembled(product, got_even, got_odd, chosen)
    rounded[...] = search[...].astype(jnp.bfloat16)


def alpha_kernel(partials, alpha, gamma):
    gamma[...], delta = unpack_two(jnp.sum(partials[...], axis=0), alpha.shape[0])
    alpha[...] = solved(delta, gamma[...])


def residual_kernel(alpha, product, got_even, got_odd, chosen, residual, new_residual, rounded):
    image = assembled(product, got_even, got_odd, chosen)
    new_residual[...] = residual[...] - combine(alpha[...], image)
    rounded[...] = new_residual[...].astype(jnp.bfloat16)


def aside_kernel(gamma, alpha, search, inverse, moved):
    k, half = moved.shape
    line, lane = places(k)
    inverse[...] = solved(gamma[...], jnp.where(line == lane, 1.0, 0.0).astype(jnp.float32))
    moved[...] = combine(alpha[...], search[:, :half])


def beta_kernel(partials, inverse, beta, gnew):
    gnew[...] = halved(unpack(jnp.sum(partials[...], axis=0), gnew.shape[0]))
    beta[...] = lax.dot_general(
        inverse[...], gnew[...], (((1,), (0,)), ((), ())), precision=HIGH, preferred_element_type=jnp.float32
    )


def search_kernel(beta, product, got_even, got_odd, chosen, search, new_search, rounded):
    new_search[...] = assembled(product, got_even, got_odd, chosen) + combine(beta[...], search[...])
    rounded[...] = new_search[...].astype(jnp.bfloat16)


def last_alpha_kernel(partials, gnew, alpha):
    delta = halved(unpack(jnp.sum(partials[...], axis=0), alpha.shape[0]))
    alpha[...] = solved(delta, gnew[...])


def last_kernel(alpha, product, from_left, chosen, residual, moved, new_search, sol, res):
    half = product.shape[1] // 2
    left = product[:, :half] + select(from_left[...], chosen[...], 1)
    res[...] = residual[:, :half] - combine(alpha[...], left)
    sol[...] = moved[...] + combine(alpha[...], new_search[:, :half])


def spread(partials):
    return lax.all_to_all(partials, AXES, 0, 0)


def shards(schur, precond, right_side, matching):
    schur_rows = schur[0]
    precond_rows = precond[0]
    start = right_side[0]
    k, face = start.shape
    size = lax.axis_size("sy")
    count = lax.axis_size("sx") * size
    tile_rows = k * k // LANES
    above = lax.pad(start, jnp.float32(0), ((0, 1, 0), (0, 0, 0)))
    below = lax.pad(matching, jnp.int32(0), ((k, 0, 0), (0, 0, 0)))
    both = above + below.astype(jnp.float32)
    following = passed_along(both, -1)
    chosen = call(chosen_kernel, bf16(face, face), both)

    def apply(rounded, matrix, weights, mode, *earlier):
        far = [partner(rounded, d) for d in range(2, size)]
        beside = partner(rounded, 1)
        rows, width = matrix.shape[0], rounded.shape[1]
        room = 2 * matrix.size + (4 << 20)
        part, rest = call(
            functools.partial(near_kernel, size), (f32(k, rows), bf16(size - 2, rows, width)), rounded, beside, matrix,
            places=[VMEM, VMEM, pl.BlockSpec(memory_space=pltpu.HBM)],
            scratch=(pltpu.VMEM((2, rows, width), jnp.bfloat16), pltpu.SemaphoreType.DMA((size,))),
            room=BUDGET - matrix.size * 7 // 4,
        )
        swap = (f32(k, face), f32(k, face))
        outs = {
            "first": (f32(k, rows), *swap, f32(k, k)),
            "both": (f32(k, rows), *swap, f32(count, 1, (tile_rows + 1) * LANES)),
            "one": (f32(k, rows), *swap, f32(count, tile_rows, LANES)),
            "last": (f32(k, rows), f32(k, face), f32(count, tile_rows, LANES)),
        }[mode]
        return call(
            functools.partial(far_kernel, len(far), mode), outs, *far, rest, part, weights, chosen, *earlier, room=room
        )

    vectors = (f32(k, 2 * face), bf16(k, 2 * face))
    residual, rounded = call(join_kernel, vectors, both, following)
    product, even, odd_, tile = apply(rounded, precond_rows, residual, "first")
    got_odd, got_even = swapped(odd_, 1), swapped(even, 0)
    search, rounded = call(direction_kernel, vectors, product, got_even, got_odd, chosen)

    product, even, odd_, partials = apply(rounded, schur_rows, search, "both", tile)
    partials = spread(partials)
    got_odd, got_even = swapped(odd_, 1), swapped(even, 0)
    alpha, gamma = call(alpha_kernel, (f32(k, k), f32(k, k)), partials)
    residual, rounded = call(residual_kernel, vectors, alpha, product, got_even, got_odd, chosen, residual)

    inverse, moved = call(aside_kernel, (f32(k, k), f32(k, face)), gamma, alpha, search)
    product, even, odd_, partials = apply(rounded, precond_rows, residual, "one")
    partials = spread(partials)
    got_odd, got_even = swapped(odd_, 1), swapped(even, 0)
    beta, gnew = call(beta_kernel, (f32(k, k), f32(k, k)), partials, inverse)
    new_search, rounded = call(search_kernel, vectors, beta, product, got_even, got_odd, chosen, search)

    product, passed, partials = apply(rounded, schur_rows, new_search, "last")
    partials = spread(partials)
    from_left = passed_along(passed, 1)
    alpha = call(last_alpha_kernel, f32(k, k), partials, gnew)
    sol, res = call(
        last_kernel, (f32(k, face), f32(k, face)),
        alpha, product, from_left, chosen, residual, moved, new_search,
    )
    return (sol[None], res[None])


def solution(mesh):
    in_specs = (P("sx", "sy", None), P("sx", "sy", None), P("sx", None, "sy"), P("sx", "sy"))
    out_specs = (P("sx", None, "sy"), P("sx", None, "sy"))
    return jax.shard_map(shards, mesh=mesh, in_specs=in_specs, out_specs=out_specs, check_vma=False)
```

profile of v0, /device:TPU:0, one launch (start us, length us, event | category | flops | bytes accessed | tf_op | source)
XLA Modules:
  0.0 92.8 jit_solution(508488804409171798)
XLA Ops:
  1.5 6.0 %collective-permute-start = (f32[33,512]{1,0:T(8,128)S(1)}, f32[33,512]{1,0:T(8,128)S(1)}, u32[]{:S(2)}, u32[]{:S(2)}) collective-permute-start(f32[33,512]{1,0:T(8,128)S(1)} %convert_add_fusion.both), channel_id=1, source_target_pairs={{4,0},{8,4},{12,8},{16,12},{20,16},{24,20},{28,24},{0,28},{5,1},{9... | collective-permute-start | bytes 202760 | tf_op jit(solution)/shard_map/ppermute | solution.py:42
  7.5 2.1 %collective-permute-done.following = f32[33,512]{1,0:T(8,128)S(1)} collective-permute-done((f32[33,512]{1,0:T(8,128)S(1)}, f32[33,512]{1,0:T(8,128)S(1)}, u32[]{:S(2)}, u32[]{:S(2)}) %collective-permute-start) | collective-permute-done | bytes 67616 | tf_op jit(solution)/shard_map/ppermute | solution.py:42
  11.8 3.5 %shard_map.60 = (f32[32,1024]{1,0:T(8,128)S(1)}, bf16[2,1024,1024]{2,1,0:T(8,128)(2,1)S(1)}) custom-call(bf16[32,1024]{1,0:T(8,128)(2,1)S(1)} %get-tuple-element.41.own, bf16[32,1024]{1,0:T(8,128)(2,1)S(1)} %collective-permute-done.3.beside, bf16[1024,4096]{1,0:T(8,128)(2,1)} %bitcast.5), custom_call_target="tpu_custom_call" | custom-call | flops 16777216 | bytes 8388608 | tf_op jit(solution)/shard_map/pallas_call | solution.py:20
  15.5 1.6 %shard_map.62 = (f32[32,1024]{1,0:T(8,128)S(1)}, f32[32,512]{1,0:T(8,128)S(1)}, f32[32,512]{1,0:T(8,128)S(1)}, f32[32,32]{1,0:T(8,128)S(1)}) custom-call(bf16[32,1024]{1,0:T(8,128)(2,1)S(1)} %collective-permute-done.1.refs_0_, bf16[32,1024]{1,0:T(8,128)(2,1)S(1)} %collective-permute-done.2.refs_1_, bf16[2,1024,1024]{2,1,0:T(8,128)(2,1)S(1)} %get-tuple-element.42.refs_2_, ...), custom_call_target="tpu_custom_call" | custom-call | flops 16777216 | bytes 8388608 | tf_op jit(solution)/shard_map/pallas_call | solution.py:20
  17.3 4.9 %collective-permute-start.5 = (f32[32,512]{1,0:T(8,128)S(1)}, f32[32,512]{1,0:T(8,128)S(1)}, u32[]{:S(2)}, u32[]{:S(2)}) collective-permute-start(f32[32,512]{1,0:T(8,128)S(1)} %get-tuple-element.47), channel_id=1, source_target_pairs={{4,8},{8,4},{12,16},{16,12},{20,24},{24,20},{28,0},{0,28},{5,9},{9... | collective-permute-start | bytes 196616 | tf_op jit(solution)/shard_map/ppermute | solution.py:51
  22.3 2.5 %collective-permute-done.5.got_odd = f32[32,512]{1,0:T(8,128)S(1)} collective-permute-done((f32[32,512]{1,0:T(8,128)S(1)}, f32[32,512]{1,0:T(8,128)S(1)}, u32[]{:S(2)}, u32[]{:S(2)}) %collective-permute-start.5) | collective-permute-done | bytes 65568 | tf_op jit(solution)/shard_map/ppermute | solution.py:51
  25.2 1.6 %collective-permute-start.6 = (bf16[32,1024]{1,0:T(8,128)(2,1)S(1)}, bf16[32,1024]{1,0:T(8,128)(2,1)S(1)}, u32[]{:S(2)}, u32[]{:S(2)}) collective-permute-start(bf16[32,1024]{1,0:T(8,128)(2,1)S(1)} %get-tuple-element.48.own), channel_id=1, source_target_pairs={{0,2},{1,3},{2,0},{3,1},{4,6},{5,7},{6,4},{7,5},{8,10},{9,11},{10,... | collective-permute-start | bytes 196616 | tf_op jit(solution)/shard_map/ppermute | solution.py:55
  27.0 3.5 %shard_map.64 = (f32[32,1024]{1,0:T(8,128)S(1)}, bf16[2,1024,1024]{2,1,0:T(8,128)(2,1)S(1)}) custom-call(bf16[32,1024]{1,0:T(8,128)(2,1)S(1)} %get-tuple-element.48.own, bf16[32,1024]{1,0:T(8,128)(2,1)S(1)} %collective-permute-done.8.beside, bf16[1024,4096]{1,0:T(8,128)(2,1)} %bitcast.7), custom_call_target="tpu_custom_call" | custom-call | flops 16777216 | bytes 8388608 | tf_op jit(solution)/shard_map/pallas_call | solution.py:20
  30.8 2.4 %shard_map.65 = (f32[32,1024]{1,0:T(8,128)S(1)}, f32[32,512]{1,0:T(8,128)S(1)}, f32[32,512]{1,0:T(8,128)S(1)}, f32[32,1,1152]{2,1,0:T(1,128)}) custom-call(bf16[32,1024]{1,0:T(8,128)(2,1)S(1)} %collective-permute-done.6.refs_0_, bf16[32,1024]{1,0:T(8,128)(2,1)S(1)} %collective-permute-done.7.refs_1_, bf16[2,1024,1024]{2,1,0:T(8,128)(2,1)S(1)} %get-tuple-element.49.refs_2_, ...), custom_call_target="tpu_custom_call" | custom-call | flops 16777216 | bytes 8388608 | tf_op jit(solution)/shard_map/pallas_call | solution.py:20
  33.2 5.5 %all-to-all-start = ((f32[32,1,1152]{2,1,0:T(1,128)}), f32[32,1,1152]{2,1,0:T(1,128)S(1)}, u32[]{:S(2)}, u32[]{:S(2)}) async-start(f32[32,1,1152]{2,1,0:T(1,128)} %get-tuple-element.53), calls=%async_computation | async-start | bytes 294912 | tf_op jit(solution)/shard_map/all_to_all | solution.py:282
  38.7 1.8 %collective-permute-start.9 = (f32[32,512]{1,0:T(8,128)S(1)}, f32[32,512]{1,0:T(8,128)S(1)}, u32[]{:S(2)}, u32[]{:S(2)}) collective-permute-start(f32[32,512]{1,0:T(8,128)S(1)} %get-tuple-element.56), channel_id=1, source_target_pairs={{0,4},{4,0},{8,12},{12,8},{16,20},{20,16},{24,28},{28,24},{1,5},{5... | collective-permute-start | bytes 196616 | tf_op jit(solution)/shard_map/ppermute | solution.py:51
  40.6 3.3 %collective-permute-start.10 = (f32[32,512]{1,0:T(8,128)S(1)}, f32[32,512]{1,0:T(8,128)S(1)}, u32[]{:S(2)}, u32[]{:S(2)}) collective-permute-start(f32[32,512]{1,0:T(8,128)S(1)} %get-tuple-element.57), channel_id=1, source_target_pairs={{4,8},{8,4},{12,16},{16,12},{20,24},{24,20},{28,0},{0,28},{5,9},{9... | collective-permute-start | bytes 196616 | tf_op jit(solution)/shard_map/ppermute | solution.py:51
  43.9 3.3 %all-to-all-done.partials = f32[32,1,1152]{2,1,0:T(1,128)S(1)} async-done(((f32[32,1,1152]{2,1,0:T(1,128)}), f32[32,1,1152]{2,1,0:T(1,128)S(1)}, u32[]{:S(2)}, u32[]{:S(2)}) %all-to-all-start) | async-done | bytes 147488 | tf_op jit(solution)/shard_map/all_to_all | solution.py:282
  51.4 3.5 %shard_map.68 = (f32[32,1024]{1,0:T(8,128)S(1)}, bf16[2,1024,1024]{2,1,0:T(8,128)(2,1)S(1)}) custom-call(bf16[32,1024]{1,0:T(8,128)(2,1)S(1)} %get-tuple-element.58.own, bf16[32,1024]{1,0:T(8,128)(2,1)S(1)} %collective-permute-done.13.beside, bf16[1024,4096]{1,0:T(8,128)(2,1)} %bitcast.6), custom_call_target="tpu_custom_call" | custom-call | flops 16777216 | bytes 8388608 | tf_op jit(solution)/shard_map/pallas_call | solution.py:20
  54.9 2.3 %shard_map.69 = (f32[32,1024]{1,0:T(8,128)S(1)}, f32[32,512]{1,0:T(8,128)S(1)}, f32[32,512]{1,0:T(8,128)S(1)}, f32[32,8,128]{2,1,0:T(8,128)}) custom-call(bf16[32,1024]{1,0:T(8,128)(2,1)S(1)} %collective-permute-done.11.refs_0_, bf16[32,1024]{1,0:T(8,128)(2,1)S(1)} %collective-permute-done.12.refs_1_, bf16[2,1024,1024]{2,1,0:T(8,128)(2,1)S(1)} %get-tuple-element.59.refs_2_, ...), custom_call_target="tpu_custom_call" | custom-call | flops 16777216 | bytes 8388608 | tf_op jit(solution)/shard_map/pallas_call | solution.py:20
  57.2 3.2 %all-to-all-start.1 = ((f32[32,8,128]{2,1,0:T(8,128)}), f32[32,8,128]{2,1,0:T(8,128)S(1)}, u32[]{:S(2)}, u32[]{:S(2)}) async-start(f32[32,8,128]{2,1,0:T(8,128)} %get-tuple-element.62), calls=%async_computation.1 | async-start | bytes 262144 | tf_op jit(solution)/shard_map/all_to_all | solution.py:282
  60.4 1.8 %collective-permute-start.14 = (f32[32,512]{1,0:T(8,128)S(1)}, f32[32,512]{1,0:T(8,128)S(1)}, u32[]{:S(2)}, u32[]{:S(2)}) collective-permute-start(f32[32,512]{1,0:T(8,128)S(1)} %get-tuple-element.67), channel_id=1, source_target_pairs={{0,4},{4,0},{8,12},{12,8},{16,20},{20,16},{24,28},{28,24},{1,5},{5... | collective-permute-start | bytes 196616 | tf_op jit(solution)/shard_map/ppermute | solution.py:51
  62.3 3.3 %collective-permute-start.15 = (f32[32,512]{1,0:T(8,128)S(1)}, f32[32,512]{1,0:T(8,128)S(1)}, u32[]{:S(2)}, u32[]{:S(2)}) collective-permute-start(f32[32,512]{1,0:T(8,128)S(1)} %get-tuple-element.68), channel_id=1, source_target_pairs={{4,8},{8,4},{12,16},{16,12},{20,24},{24,20},{28,0},{0,28},{5,9},{9... | collective-permute-start | bytes 196616 | tf_op jit(solution)/shard_map/ppermute | solution.py:51
  66.8 2.0 %all-to-all-done.1.partials = f32[32,8,128]{2,1,0:T(8,128)S(1)} async-done(((f32[32,8,128]{2,1,0:T(8,128)}), f32[32,8,128]{2,1,0:T(8,128)S(1)}, u32[]{:S(2)}, u32[]{:S(2)}) %all-to-all-start.1) | async-done | bytes 131104 | tf_op jit(solution)/shard_map/all_to_all | solution.py:282
  72.0 3.5 %shard_map.73 = (f32[32,1024]{1,0:T(8,128)S(1)}, bf16[2,1024,1024]{2,1,0:T(8,128)(2,1)S(1)}) custom-call(bf16[32,1024]{1,0:T(8,128)(2,1)S(1)} %get-tuple-element.69.own, bf16[32,1024]{1,0:T(8,128)(2,1)S(1)} %collective-permute-done.18.beside, bf16[1024,4096]{1,0:T(8,128)(2,1)} %bitcast.8), custom_call_target="tpu_custom_call" | custom-call | flops 16777216 | bytes 8388608 | tf_op jit(solution)/shard_map/pallas_call | solution.py:20
  75.7 2.3 %shard_map.74 = (f32[32,1024]{1,0:T(8,128)S(1)}, f32[32,512]{1,0:T(8,128)S(1)}, f32[32,8,128]{2,1,0:T(8,128)}) custom-call(bf16[32,1024]{1,0:T(8,128)(2,1)S(1)} %collective-permute-done.16.refs_0_, bf16[32,1024]{1,0:T(8,128)(2,1)S(1)} %collective-permute-done.17.refs_1_, bf16[2,1024,1024]{2,1,0:T(8,128)(2,1)S(1)} %get-tuple-element.70.refs_2_, ...), custom_call_target="tpu_custom_call" | custom-call | flops 16777216 | bytes 8388608 | tf_op jit(solution)/shard_map/pallas_call | solution.py:20
  78.0 4.0 %all-to-all-start.2 = ((f32[32,8,128]{2,1,0:T(8,128)}), f32[32,8,128]{2,1,0:T(8,128)S(1)}, u32[]{:S(2)}, u32[]{:S(2)}) async-start(f32[32,8,128]{2,1,0:T(8,128)} %get-tuple-element.73), calls=%async_computation.2 | async-start | bytes 262144 | tf_op jit(solution)/shard_map/all_to_all | solution.py:282
  82.0 1.8 %collective-permute-start.19 = (f32[32,512]{1,0:T(8,128)S(1)}, f32[32,512]{1,0:T(8,128)S(1)}, u32[]{:S(2)}, u32[]{:S(2)}) collective-permute-start(f32[32,512]{1,0:T(8,128)S(1)} %get-tuple-element.76), channel_id=1, source_target_pairs={{28,0},{0,4},{4,8},{8,12},{12,16},{16,20},{20,24},{24,28},{29,1},{... | collective-permute-start | bytes 196616 | tf_op jit(solution)/shard_map/ppermute | solution.py:42
  83.8 6.5 %all-to-all-done.2.partials = f32[32,8,128]{2,1,0:T(8,128)S(1)} async-done(((f32[32,8,128]{2,1,0:T(8,128)}), f32[32,8,128]{2,1,0:T(8,128)S(1)}, u32[]{:S(2)}, u32[]{:S(2)}) %all-to-all-start.2) | async-done | bytes 131104 | tf_op jit(solution)/shard_map/all_to_all | solution.py:282
  (41 shorter events, 15.5 us)
Async XLA Ops:
  1.5 8.1 %collective-permute-start = (f32[33,512]{1,0:T(8,128)S(1)}, f32[33,512]{1,0:T(8,128)S(1)}, u32[]{:S(2)}, u32[]{:S(2)}) collective-permute-start(f32[33,512]{1,0:T(8,128)S(1)} %convert_add_fusion.both), channel_id=1, source_target_pairs={{4,0},{8,4},{12,8},{16,12},{20,16},{24,20},{28,24},{0,28},{5,1},{9... | collective-permute-start | bytes 202760 | tf_op jit(solution)/shard_map/ppermute | solution.py:42
  9.8 2.0 %collective-permute-start.3 = (bf16[32,1024]{1,0:T(8,128)(2,1)S(1)}, bf16[32,1024]{1,0:T(8,128)(2,1)S(1)}, u32[]{:S(2)}, u32[]{:S(2)}) collective-permute-start(bf16[32,1024]{1,0:T(8,128)(2,1)S(1)} %get-tuple-element.41.own), channel_id=1, source_target_pairs={{0,1},{1,0},{2,3},{3,2},{4,5},{5,4},{6,7},{7,6},{8,9},{9,8},{10,11... | collective-permute-start | bytes 196616 | tf_op jit(solution)/shard_map/ppermute | solution.py:55
  9.8 5.5 %collective-permute-start.1 = (bf16[32,1024]{1,0:T(8,128)(2,1)S(1)}, bf16[32,1024]{1,0:T(8,128)(2,1)S(1)}, u32[]{:S(2)}, u32[]{:S(2)}) collective-permute-start(bf16[32,1024]{1,0:T(8,128)(2,1)S(1)} %get-tuple-element.41.own), channel_id=1, source_target_pairs={{0,2},{1,3},{2,0},{3,1},{4,6},{5,7},{6,4},{7,5},{8,10},{9,11},{10,... | collective-permute-start | bytes 196616 | tf_op jit(solution)/shard_map/ppermute | solution.py:55
  11.4 4.1 %collective-permute-start.2 = (bf16[32,1024]{1,0:T(8,128)(2,1)S(1)}, bf16[32,1024]{1,0:T(8,128)(2,1)S(1)}, u32[]{:S(2)}, u32[]{:S(2)}) collective-permute-start(bf16[32,1024]{1,0:T(8,128)(2,1)S(1)} %get-tuple-element.41.own), channel_id=1, source_target_pairs={{0,3},{1,2},{2,1},{3,0},{4,7},{5,6},{6,5},{7,4},{8,11},{9,10},{10,... | collective-permute-start | bytes 196616 | tf_op jit(solution)/shard_map/ppermute | solution.py:55
  17.1 5.2 %collective-permute-start.4 = (f32[32,512]{1,0:T(8,128)S(1)}, f32[32,512]{1,0:T(8,128)S(1)}, u32[]{:S(2)}, u32[]{:S(2)}) collective-permute-start(f32[32,512]{1,0:T(8,128)S(1)} %get-tuple-element.46), channel_id=1, source_target_pairs={{0,4},{4,0},{8,12},{12,8},{16,20},{20,16},{24,28},{28,24},{1,5},{5... | collective-permute-start | bytes 196616 | tf_op jit(solution)/shard_map/ppermute | solution.py:51
  17.3 7.4 %collective-permute-start.5 = (f32[32,512]{1,0:T(8,128)S(1)}, f32[32,512]{1,0:T(8,128)S(1)}, u32[]{:S(2)}, u32[]{:S(2)}) collective-permute-start(f32[32,512]{1,0:T(8,128)S(1)} %get-tuple-element.47), channel_id=1, source_target_pairs={{4,8},{8,4},{12,16},{16,12},{20,24},{24,20},{28,0},{0,28},{5,9},{9... | collective-permute-start | bytes 196616 | tf_op jit(solution)/shard_map/ppermute | solution.py:51
  25.1 1.9 %collective-permute-start.8 = (bf16[32,1024]{1,0:T(8,128)(2,1)S(1)}, bf16[32,1024]{1,0:T(8,128)(2,1)S(1)}, u32[]{:S(2)}, u32[]{:S(2)}) collective-permute-start(bf16[32,1024]{1,0:T(8,128)(2,1)S(1)} %get-tuple-element.48.own), channel_id=1, source_target_pairs={{0,1},{1,0},{2,3},{3,2},{4,5},{5,4},{6,7},{7,6},{8,9},{9,8},{10,11... | collective-permute-start | bytes 196616 | tf_op jit(solution)/shard_map/ppermute | solution.py:55
  25.2 5.4 %collective-permute-start.6 = (bf16[32,1024]{1,0:T(8,128)(2,1)S(1)}, bf16[32,1024]{1,0:T(8,128)(2,1)S(1)}, u32[]{:S(2)}, u32[]{:S(2)}) collective-permute-start(bf16[32,1024]{1,0:T(8,128)(2,1)S(1)} %get-tuple-element.48.own), channel_id=1, source_target_pairs={{0,2},{1,3},{2,0},{3,1},{4,6},{5,7},{6,4},{7,5},{8,10},{9,11},{10,... | collective-permute-start | bytes 196616 | tf_op jit(solution)/shard_map/ppermute | solution.py:55
  26.7 4.1 %collective-permute-start.7 = (bf16[32,1024]{1,0:T(8,128)(2,1)S(1)}, bf16[32,1024]{1,0:T(8,128)(2,1)S(1)}, u32[]{:S(2)}, u32[]{:S(2)}) collective-permute-start(bf16[32,1024]{1,0:T(8,128)(2,1)S(1)} %get-tuple-element.48.own), channel_id=1, source_target_pairs={{0,3},{1,2},{2,1},{3,0},{4,7},{5,6},{6,5},{7,4},{8,11},{9,10},{10,... | collective-permute-start | bytes 196616 | tf_op jit(solution)/shard_map/ppermute | solution.py:55
  33.2 14.0 %all-to-all-start = ((f32[32,1,1152]{2,1,0:T(1,128)}), f32[32,1,1152]{2,1,0:T(1,128)S(1)}, u32[]{:S(2)}, u32[]{:S(2)}) async-start(f32[32,1,1152]{2,1,0:T(1,128)} %get-tuple-element.53), calls=%async_computation | async-start | bytes 294912 | tf_op jit(solution)/shard_map/all_to_all | solution.py:282
  38.7 9.9 %collective-permute-start.9 = (f32[32,512]{1,0:T(8,128)S(1)}, f32[32,512]{1,0:T(8,128)S(1)}, u32[]{:S(2)}, u32[]{:S(2)}) collective-permute-start(f32[32,512]{1,0:T(8,128)S(1)} %get-tuple-element.56), channel_id=1, source_target_pairs={{0,4},{4,0},{8,12},{12,8},{16,20},{20,16},{24,28},{28,24},{1,5},{5... | collective-permute-start | bytes 196616 | tf_op jit(solution)/shard_map/ppermute | solution.py:51
  40.6 8.0 %collective-permute-start.10 = (f32[32,512]{1,0:T(8,128)S(1)}, f32[32,512]{1,0:T(8,128)S(1)}, u32[]{:S(2)}, u32[]{:S(2)}) collective-permute-start(f32[32,512]{1,0:T(8,128)S(1)} %get-tuple-element.57), channel_id=1, source_target_pairs={{4,8},{8,4},{12,16},{16,12},{20,24},{24,20},{28,0},{0,28},{5,9},{9... | collective-permute-start | bytes 196616 | tf_op jit(solution)/shard_map/ppermute | solution.py:51
  49.1 2.3 %collective-permute-start.13 = (bf16[32,1024]{1,0:T(8,128)(2,1)S(1)}, bf16[32,1024]{1,0:T(8,128)(2,1)S(1)}, u32[]{:S(2)}, u32[]{:S(2)}) collective-permute-start(bf16[32,1024]{1,0:T(8,128)(2,1)S(1)} %get-tuple-element.58.own), channel_id=1, source_target_pairs={{0,1},{1,0},{2,3},{3,2},{4,5},{5,4},{6,7},{7,6},{8,9},{9,8},{10,11... | collective-permute-start | bytes 196616 | tf_op jit(solution)/shard_map/ppermute | solution.py:55
  50.0 5.0 %collective-permute-start.11 = (bf16[32,1024]{1,0:T(8,128)(2,1)S(1)}, bf16[32,1024]{1,0:T(8,128)(2,1)S(1)}, u32[]{:S(2)}, u32[]{:S(2)}) collective-permute-start(bf16[32,1024]{1,0:T(8,128)(2,1)S(1)} %get-tuple-element.58.own), channel_id=1, source_target_pairs={{0,2},{1,3},{2,0},{3,1},{4,6},{5,7},{6,4},{7,5},{8,10},{9,11},{10,... | collective-permute-start | bytes 196616 | tf_op jit(solution)/shard_map/ppermute | solution.py:55
  50.3 4.7 %collective-permute-start.12 = (bf16[32,1024]{1,0:T(8,128)(2,1)S(1)}, bf16[32,1024]{1,0:T(8,128)(2,1)S(1)}, u32[]{:S(2)}, u32[]{:S(2)}) collective-permute-start(bf16[32,1024]{1,0:T(8,128)(2,1)S(1)} %get-tuple-element.58.own), channel_id=1, source_target_pairs={{0,3},{1,2},{2,1},{3,0},{4,7},{5,6},{6,5},{7,4},{8,11},{9,10},{10,... | collective-permute-start | bytes 196616 | tf_op jit(solution)/shard_map/ppermute | solution.py:55
  57.2 11.5 %all-to-all-start.1 = ((f32[32,8,128]{2,1,0:T(8,128)}), f32[32,8,128]{2,1,0:T(8,128)S(1)}, u32[]{:S(2)}, u32[]{:S(2)}) async-start(f32[32,8,128]{2,1,0:T(8,128)} %get-tuple-element.62), calls=%async_computation.1 | async-start | bytes 262144 | tf_op jit(solution)/shard_map/all_to_all | solution.py:282
  60.4 8.7 %collective-permute-start.14 = (f32[32,512]{1,0:T(8,128)S(1)}, f32[32,512]{1,0:T(8,128)S(1)}, u32[]{:S(2)}, u32[]{:S(2)}) collective-permute-start(f32[32,512]{1,0:T(8,128)S(1)} %get-tuple-element.67), channel_id=1, source_target_pairs={{0,4},{4,0},{8,12},{12,8},{16,20},{20,16},{24,28},{28,24},{1,5},{5... | collective-permute-start | bytes 196616 | tf_op jit(solution)/shard_map/ppermute | solution.py:51
  62.3 7.4 %collective-permute-start.15 = (f32[32,512]{1,0:T(8,128)S(1)}, f32[32,512]{1,0:T(8,128)S(1)}, u32[]{:S(2)}, u32[]{:S(2)}) collective-permute-start(f32[32,512]{1,0:T(8,128)S(1)} %get-tuple-element.68), channel_id=1, source_target_pairs={{4,8},{8,4},{12,16},{16,12},{20,24},{24,20},{28,0},{0,28},{5,9},{9... | collective-permute-start | bytes 196616 | tf_op jit(solution)/shard_map/ppermute | solution.py:51
  70.0 1.9 %collective-permute-start.18 = (bf16[32,1024]{1,0:T(8,128)(2,1)S(1)}, bf16[32,1024]{1,0:T(8,128)(2,1)S(1)}, u32[]{:S(2)}, u32[]{:S(2)}) collective-permute-start(bf16[32,1024]{1,0:T(8,128)(2,1)S(1)} %get-tuple-element.69.own), channel_id=1, source_target_pairs={{0,1},{1,0},{2,3},{3,2},{4,5},{5,4},{6,7},{7,6},{8,9},{9,8},{10,11... | collective-permute-start | bytes 196616 | tf_op jit(solution)/shard_map/ppermute | solution.py:55
  70.2 5.3 %collective-permute-start.16 = (bf16[32,1024]{1,0:T(8,128)(2,1)S(1)}, bf16[32,1024]{1,0:T(8,128)(2,1)S(1)}, u32[]{:S(2)}, u32[]{:S(2)}) collective-permute-start(bf16[32,1024]{1,0:T(8,128)(2,1)S(1)} %get-tuple-element.69.own), channel_id=1, source_target_pairs={{0,2},{1,3},{2,0},{3,1},{4,6},{5,7},{6,4},{7,5},{8,10},{9,11},{10,... | collective-permute-start | bytes 196616 | tf_op jit(solution)/shard_map/ppermute | solution.py:55
  71.6 4.1 %collective-permute-start.17 = (bf16[32,1024]{1,0:T(8,128)(2,1)S(1)}, bf16[32,1024]{1,0:T(8,128)(2,1)S(1)}, u32[]{:S(2)}, u32[]{:S(2)}) collective-permute-start(bf16[32,1024]{1,0:T(8,128)(2,1)S(1)} %get-tuple-element.69.own), channel_id=1, source_target_pairs={{0,3},{1,2},{2,1},{3,0},{4,7},{5,6},{6,5},{7,4},{8,11},{9,10},{10,... | collective-permute-start | bytes 196616 | tf_op jit(solution)/shard_map/ppermute | solution.py:55
  78.0 12.4 %all-to-all-start.2 = ((f32[32,8,128]{2,1,0:T(8,128)}), f32[32,8,128]{2,1,0:T(8,128)S(1)}, u32[]{:S(2)}, u32[]{:S(2)}) async-start(f32[32,8,128]{2,1,0:T(8,128)} %get-tuple-element.73), calls=%async_computation.2 | async-start | bytes 262144 | tf_op jit(solution)/shard_map/all_to_all | solution.py:282
  82.0 9.6 %collective-permute-start.19 = (f32[32,512]{1,0:T(8,128)S(1)}, f32[32,512]{1,0:T(8,128)S(1)}, u32[]{:S(2)}, u32[]{:S(2)}) collective-permute-start(f32[32,512]{1,0:T(8,128)S(1)} %get-tuple-element.76), channel_id=1, source_target_pairs={{28,0},{0,4},{4,8},{8,12},{12,16},{16,20},{20,24},{24,28},{29,1},{... | collective-permute-start | bytes 196616 | tf_op jit(solution)/shard_map/ppermute | solution.py:42
where the time goes:
time: 93.3 us; the launch traced here: 92.8 us
  starting transfers between devices  44 us (47%)
  Pallas kernels  29.6 us (32%)
  waiting for transfers between devices  17.6 us (19%)
    pallas_call x18, Pallas kernels, call(): pl.pallas_call(body, out_shape=outs, in_specs=places or [VMEM] * len(args...  29.6 us
    ppermute x6, starting transfers between devices, swapped(): return lax.ppermute(block, 'sx', route)  15.5 us
    all_to_all x3, starting transfers between devices, spread(): return lax.all_to_all(partials, AXES, 0, 0)  12.7 us
    all_to_all x3, waiting for transfers between devices, spread(): return lax.all_to_all(partials, AXES, 0, 0)  11.9 us
    ppermute x12, starting transfers between devices, partner(): lax.ppermute(block, 'sy', [(i, i ^ distance) for i in range(lax.axis_size...  7.98 us
    ppermute x2, starting transfers between devices, passed_along(): return lax.ppermute(block, 'sx', route)  7.85 us
    ppermute x6, waiting for transfers between devices, swapped(): return lax.ppermute(block, 'sx', route)  3.09 us
    ppermute x2, waiting for transfers between devices, passed_along(): return lax.ppermute(block, 'sx', route)  2.06 us
  transfers between devices with their start and end apart: 23, of which 9 were waited for; matrix products, arithmetic and copies ran while one was open for 0% of the time, Pallas kernels for 20%

commit v1 on v0

--- a/solution.py
+++ b/solution.py
@@ -113,6 +113,19 @@
     return upper, lower
 
 
+def pair(a, b, c, d):
+    over_a = 1.0 / a
+    ratio = b * over_a
+    over_d = 1.0 / (d - c * ratio)
+
+    def solve(x, y):
+        x = x * over_a
+        y = (y - c * x) * over_d
+        return x - ratio * y, y
+
+    return solve
+
+
 def solved(matrix, sides):
     k = matrix.shape[0]
     table = jnp.concatenate([matrix, sides, jnp.zeros((k, LANES - 2 * k), jnp.float32)], axis=1)
@@ -121,19 +134,15 @@
         columns = [jnp.broadcast_to(table[:, step + i : step + i + 1], table.shape) for i in range(4)]
         rows = [table[step + i : step + i + 1] for i in range(4)]
         block = [[columns[j][step + i : step + i + 1] for j in range(4)] for i in range(4)]
-        (a, b), (c, d) = block[0][:2], block[1][:2]
-        scale = 1.0 / (a * d - b * c)
-
-        def upper(x, y):
-            return (d * x - b * y) * scale, (a * y - c * x) * scale
-
+        upper = pair(*block[0][:2], *block[1][:2])
         sides = [upper(block[0][j], block[1][j]) for j in (2, 3)]
         first = upper(rows[0], rows[1])
-        lower = [[block[i][j] - (block[i][0] * sides[j - 2][0] + block[i][1] * sides[j - 2][1]) for j in (2, 3)] for i in (2, 3)]
+        lower = [
+            [block[i][j] - (block[i][0] * sides[j - 2][0] + block[i][1] * sides[j - 2][1]) for j in (2, 3)]
+            for i in (2, 3)
+        ]
         rest = [rows[i] - (block[i][0] * first[0] + block[i][1] * first[1]) for i in (2, 3)]
-        scale = 1.0 / (lower[0][0] * lower[1][1] - lower[0][1] * lower[1][0])
-        third = (lower[1][1] * rest[0] - lower[0][1] * rest[1]) * scale
-        fourth = (lower[0][0] * rest[1] - lower[1][0] * rest[0]) * scale
+        third, fourth = pair(*lower[0], *lower[1])(*rest)
         new = [first[i] - (sides[0][i] * third + sides[1][i] * fourth) for i in (0, 1)] + [third, fourth]
         table = table - (columns[0] * new[0] + columns[1] * new[1]) - (columns[2] * new[2] + columns[3] * new[3])
         for i in range(4):

time: 93.3 us -> 93.5 us (level)
  no operation moved by 1% of the time
where the time goes in v1:
time: 93.5 us; the launch traced here: 93 us
  starting transfers between devices  43.8 us (47%)
  Pallas kernels  30.2 us (32%)
  waiting for transfers between devices  17.3 us (19%)
    pallas_call x18, Pallas kernels, call(): pl.pallas_call(body, out_shape=outs, in_specs=places or [VMEM] * len(args...  30.2 us
    ppermute x6, starting transfers between devices, swapped(): return lax.ppermute(block, 'sx', route)  15.5 us
    all_to_all x3, starting transfers between devices, spread(): return lax.all_to_all(partials, AXES, 0, 0)  12.5 us
    all_to_all x3, waiting for transfers between devices, spread(): return lax.all_to_all(partials, AXES, 0, 0)  11.7 us
    ppermute x12, starting transfers between devices, partner(): lax.ppermute(block, 'sy', [(i, i ^ distance) for i in range(lax.axis_size...  7.98 us
    ppermute x2, starting transfers between devices, passed_along(): return lax.ppermute(block, 'sx', route)  7.85 us
    ppermute x6, waiting for transfers between devices, swapped(): return lax.ppermute(block, 'sx', route)  3.09 us
    ppermute x2, waiting for transfers between devices, passed_along(): return lax.ppermute(block, 'sx', route)  2.06 us
  transfers between devices with their start and end apart: 23, of which 9 were waited for; matrix products, arithmetic and copies ran while one was open for 0% of the time, Pallas kernels for 20%

profile of v1, /device:TPU:0, one launch (start us, length us, event | category | flops | bytes accessed | tf_op | source)
XLA Modules:
  0.0 93.0 jit_solution(17555264353950481512)
XLA Ops:
  1.5 6.0 %collective-permute-start = (f32[33,512]{1,0:T(8,128)S(1)}, f32[33,512]{1,0:T(8,128)S(1)}, u32[]{:S(2)}, u32[]{:S(2)}) collective-permute-start(f32[33,512]{1,0:T(8,128)S(1)} %convert_add_fusion.both), channel_id=1, source_target_pairs={{4,0},{8,4},{12,8},{16,12},{20,16},{24,20},{28,24},{0,28},{5,1},{9... | collective-permute-start | bytes 202760 | tf_op jit(solution)/shard_map/ppermute | solution.py:42
  7.5 2.1 %collective-permute-done.following = f32[33,512]{1,0:T(8,128)S(1)} collective-permute-done((f32[33,512]{1,0:T(8,128)S(1)}, f32[33,512]{1,0:T(8,128)S(1)}, u32[]{:S(2)}, u32[]{:S(2)}) %collective-permute-start) | collective-permute-done | bytes 67616 | tf_op jit(solution)/shard_map/ppermute | solution.py:42
  11.8 3.5 %shard_map.60 = (f32[32,1024]{1,0:T(8,128)S(1)}, bf16[2,1024,1024]{2,1,0:T(8,128)(2,1)S(1)}) custom-call(bf16[32,1024]{1,0:T(8,128)(2,1)S(1)} %get-tuple-element.41.own, bf16[32,1024]{1,0:T(8,128)(2,1)S(1)} %collective-permute-done.3.beside, bf16[1024,4096]{1,0:T(8,128)(2,1)} %bitcast.5), custom_call_target="tpu_custom_call" | custom-call | flops 16777216 | bytes 8388608 | tf_op jit(solution)/shard_map/pallas_call | solution.py:20
  15.5 1.6 %shard_map.62 = (f32[32,1024]{1,0:T(8,128)S(1)}, f32[32,512]{1,0:T(8,128)S(1)}, f32[32,512]{1,0:T(8,128)S(1)}, f32[32,32]{1,0:T(8,128)S(1)}) custom-call(bf16[32,1024]{1,0:T(8,128)(2,1)S(1)} %collective-permute-done.1.refs_0_, bf16[32,1024]{1,0:T(8,128)(2,1)S(1)} %collective-permute-done.2.refs_1_, bf16[2,1024,1024]{2,1,0:T(8,128)(2,1)S(1)} %get-tuple-element.42.refs_2_, ...), custom_call_target="tpu_custom_call" | custom-call | flops 16777216 | bytes 8388608 | tf_op jit(solution)/shard_map/pallas_call | solution.py:20
  17.3 4.9 %collective-permute-start.5 = (f32[32,512]{1,0:T(8,128)S(1)}, f32[32,512]{1,0:T(8,128)S(1)}, u32[]{:S(2)}, u32[]{:S(2)}) collective-permute-start(f32[32,512]{1,0:T(8,128)S(1)} %get-tuple-element.47), channel_id=1, source_target_pairs={{4,8},{8,4},{12,16},{16,12},{20,24},{24,20},{28,0},{0,28},{5,9},{9... | collective-permute-start | bytes 196616 | tf_op jit(solution)/shard_map/ppermute | solution.py:51
  22.3 2.5 %collective-permute-done.5.got_odd = f32[32,512]{1,0:T(8,128)S(1)} collective-permute-done((f32[32,512]{1,0:T(8,128)S(1)}, f32[32,512]{1,0:T(8,128)S(1)}, u32[]{:S(2)}, u32[]{:S(2)}) %collective-permute-start.5) | collective-permute-done | bytes 65568 | tf_op jit(solution)/shard_map/ppermute | solution.py:51
  27.0 3.5 %shard_map.64 = (f32[32,1024]{1,0:T(8,128)S(1)}, bf16[2,1024,1024]{2,1,0:T(8,128)(2,1)S(1)}) custom-call(bf16[32,1024]{1,0:T(8,128)(2,1)S(1)} %get-tuple-element.48.own, bf16[32,1024]{1,0:T(8,128)(2,1)S(1)} %collective-permute-done.8.beside, bf16[1024,4096]{1,0:T(8,128)(2,1)} %bitcast.7), custom_call_target="tpu_custom_call" | custom-call | flops 16777216 | bytes 8388608 | tf_op jit(solution)/shard_map/pallas_call | solution.py:20
  30.8 2.4 %shard_map.65 = (f32[32,1024]{1,0:T(8,128)S(1)}, f32[32,512]{1,0:T(8,128)S(1)}, f32[32,512]{1,0:T(8,128)S(1)}, f32[32,1,1152]{2,1,0:T(1,128)}) custom-call(bf16[32,1024]{1,0:T(8,128)(2,1)S(1)} %collective-permute-done.6.refs_0_, bf16[32,1024]{1,0:T(8,128)(2,1)S(1)} %collective-permute-done.7.refs_1_, bf16[2,1024,1024]{2,1,0:T(8,128)(2,1)S(1)} %get-tuple-element.49.refs_2_, ...), custom_call_target="tpu_custom_call" | custom-call | flops 16777216 | bytes 8388608 | tf_op jit(solution)/shard_map/pallas_call | solution.py:20
  33.2 5.5 %all-to-all-start = ((f32[32,1,1152]{2,1,0:T(1,128)}), f32[32,1,1152]{2,1,0:T(1,128)S(1)}, u32[]{:S(2)}, u32[]{:S(2)}) async-start(f32[32,1,1152]{2,1,0:T(1,128)} %get-tuple-element.53), calls=%async_computation | async-start | bytes 294912 | tf_op jit(solution)/shard_map/all_to_all | solution.py:291
  38.7 1.8 %collective-permute-start.9 = (f32[32,512]{1,0:T(8,128)S(1)}, f32[32,512]{1,0:T(8,128)S(1)}, u32[]{:S(2)}, u32[]{:S(2)}) collective-permute-start(f32[32,512]{1,0:T(8,128)S(1)} %get-tuple-element.56), channel_id=1, source_target_pairs={{0,4},{4,0},{8,12},{12,8},{16,20},{20,16},{24,28},{28,24},{1,5},{5... | collective-permute-start | bytes 196616 | tf_op jit(solution)/shard_map/ppermute | solution.py:51
  40.6 3.3 %collective-permute-start.10 = (f32[32,512]{1,0:T(8,128)S(1)}, f32[32,512]{1,0:T(8,128)S(1)}, u32[]{:S(2)}, u32[]{:S(2)}) collective-permute-start(f32[32,512]{1,0:T(8,128)S(1)} %get-tuple-element.57), channel_id=1, source_target_pairs={{4,8},{8,4},{12,16},{16,12},{20,24},{24,20},{28,0},{0,28},{5,9},{9... | collective-permute-start | bytes 196616 | tf_op jit(solution)/shard_map/ppermute | solution.py:51
  43.9 3.3 %all-to-all-done.partials = f32[32,1,1152]{2,1,0:T(1,128)S(1)} async-done(((f32[32,1,1152]{2,1,0:T(1,128)}), f32[32,1,1152]{2,1,0:T(1,128)S(1)}, u32[]{:S(2)}, u32[]{:S(2)}) %all-to-all-start) | async-done | bytes 147488 | tf_op jit(solution)/shard_map/all_to_all | solution.py:291
  47.2 1.6 %shard_map.66 = (f32[32,32]{1,0:T(8,128)S(1)}, f32[32,32]{1,0:T(8,128)S(1)}) custom-call(f32[32,1,1152]{2,1,0:T(1,128)S(1)} %all-to-all-done.partials), custom_call_target="tpu_custom_call" | custom-call | flops 16777216 | bytes 8388608 | tf_op jit(solution)/shard_map/pallas_call | solution.py:20
  51.6 3.5 %shard_map.68 = (f32[32,1024]{1,0:T(8,128)S(1)}, bf16[2,1024,1024]{2,1,0:T(8,128)(2,1)S(1)}) custom-call(bf16[32,1024]{1,0:T(8,128)(2,1)S(1)} %get-tuple-element.58.own, bf16[32,1024]{1,0:T(8,128)(2,1)S(1)} %collective-permute-done.13.beside, bf16[1024,4096]{1,0:T(8,128)(2,1)} %bitcast.6), custom_call_target="tpu_custom_call" | custom-call | flops 16777216 | bytes 8388608 | tf_op jit(solution)/shard_map/pallas_call | solution.py:20
  55.2 2.3 %shard_map.69 = (f32[32,1024]{1,0:T(8,128)S(1)}, f32[32,512]{1,0:T(8,128)S(1)}, f32[32,512]{1,0:T(8,128)S(1)}, f32[32,8,128]{2,1,0:T(8,128)}) custom-call(bf16[32,1024]{1,0:T(8,128)(2,1)S(1)} %collective-permute-done.11.refs_0_, bf16[32,1024]{1,0:T(8,128)(2,1)S(1)} %collective-permute-done.12.refs_1_, bf16[2,1024,1024]{2,1,0:T(8,128)(2,1)S(1)} %get-tuple-element.59.refs_2_, ...), custom_call_target="tpu_custom_call" | custom-call | flops 16777216 | bytes 8388608 | tf_op jit(solution)/shard_map/pallas_call | solution.py:20
  57.4 3.0 %all-to-all-start.1 = ((f32[32,8,128]{2,1,0:T(8,128)}), f32[32,8,128]{2,1,0:T(8,128)S(1)}, u32[]{:S(2)}, u32[]{:S(2)}) async-start(f32[32,8,128]{2,1,0:T(8,128)} %get-tuple-element.62), calls=%async_computation.1 | async-start | bytes 262144 | tf_op jit(solution)/shard_map/all_to_all | solution.py:291
  60.4 1.8 %collective-permute-start.14 = (f32[32,512]{1,0:T(8,128)S(1)}, f32[32,512]{1,0:T(8,128)S(1)}, u32[]{:S(2)}, u32[]{:S(2)}) collective-permute-start(f32[32,512]{1,0:T(8,128)S(1)} %get-tuple-element.67), channel_id=1, source_target_pairs={{0,4},{4,0},{8,12},{12,8},{16,20},{20,16},{24,28},{28,24},{1,5},{5... | collective-permute-start | bytes 196616 | tf_op jit(solution)/shard_map/ppermute | solution.py:51
  62.3 3.3 %collective-permute-start.15 = (f32[32,512]{1,0:T(8,128)S(1)}, f32[32,512]{1,0:T(8,128)S(1)}, u32[]{:S(2)}, u32[]{:S(2)}) collective-permute-start(f32[32,512]{1,0:T(8,128)S(1)} %get-tuple-element.68), channel_id=1, source_target_pairs={{4,8},{8,4},{12,16},{16,12},{20,24},{24,20},{28,0},{0,28},{5,9},{9... | collective-permute-start | bytes 196616 | tf_op jit(solution)/shard_map/ppermute | solution.py:51
  67.0 1.8 %all-to-all-done.1.partials = f32[32,8,128]{2,1,0:T(8,128)S(1)} async-done(((f32[32,8,128]{2,1,0:T(8,128)}), f32[32,8,128]{2,1,0:T(8,128)S(1)}, u32[]{:S(2)}, u32[]{:S(2)}) %all-to-all-start.1) | async-done | bytes 131104 | tf_op jit(solution)/shard_map/all_to_all | solution.py:291
  72.0 3.5 %shard_map.73 = (f32[32,1024]{1,0:T(8,128)S(1)}, bf16[2,1024,1024]{2,1,0:T(8,128)(2,1)S(1)}) custom-call(bf16[32,1024]{1,0:T(8,128)(2,1)S(1)} %get-tuple-element.69.own, bf16[32,1024]{1,0:T(8,128)(2,1)S(1)} %collective-permute-done.18.beside, bf16[1024,4096]{1,0:T(8,128)(2,1)} %bitcast.8), custom_call_target="tpu_custom_call" | custom-call | flops 16777216 | bytes 8388608 | tf_op jit(solution)/shard_map/pallas_call | solution.py:20
  75.7 2.3 %shard_map.74 = (f32[32,1024]{1,0:T(8,128)S(1)}, f32[32,512]{1,0:T(8,128)S(1)}, f32[32,8,128]{2,1,0:T(8,128)}) custom-call(bf16[32,1024]{1,0:T(8,128)(2,1)S(1)} %collective-permute-done.16.refs_0_, bf16[32,1024]{1,0:T(8,128)(2,1)S(1)} %collective-permute-done.17.refs_1_, bf16[2,1024,1024]{2,1,0:T(8,128)(2,1)S(1)} %get-tuple-element.70.refs_2_, ...), custom_call_target="tpu_custom_call" | custom-call | flops 16777216 | bytes 8388608 | tf_op jit(solution)/shard_map/pallas_call | solution.py:20
  78.0 4.0 %all-to-all-start.2 = ((f32[32,8,128]{2,1,0:T(8,128)}), f32[32,8,128]{2,1,0:T(8,128)S(1)}, u32[]{:S(2)}, u32[]{:S(2)}) async-start(f32[32,8,128]{2,1,0:T(8,128)} %get-tuple-element.73), calls=%async_computation.2 | async-start | bytes 262144 | tf_op jit(solution)/shard_map/all_to_all | solution.py:291
  82.0 1.8 %collective-permute-start.19 = (f32[32,512]{1,0:T(8,128)S(1)}, f32[32,512]{1,0:T(8,128)S(1)}, u32[]{:S(2)}, u32[]{:S(2)}) collective-permute-start(f32[32,512]{1,0:T(8,128)S(1)} %get-tuple-element.76), channel_id=1, source_target_pairs={{28,0},{0,4},{4,8},{8,12},{12,16},{16,20},{20,24},{24,28},{29,1},{... | collective-permute-start | bytes 196616 | tf_op jit(solution)/shard_map/ppermute | solution.py:42
  83.8 6.5 %all-to-all-done.2.partials = f32[32,8,128]{2,1,0:T(8,128)S(1)} async-done(((f32[32,8,128]{2,1,0:T(8,128)}), f32[32,8,128]{2,1,0:T(8,128)S(1)}, u32[]{:S(2)}, u32[]{:S(2)}) %all-to-all-start.2) | async-done | bytes 131104 | tf_op jit(solution)/shard_map/all_to_all | solution.py:291
  (41 shorter events, 16.1 us)
Async XLA Ops:
  1.5 8.1 %collective-permute-start = (f32[33,512]{1,0:T(8,128)S(1)}, f32[33,512]{1,0:T(8,128)S(1)}, u32[]{:S(2)}, u32[]{:S(2)}) collective-permute-start(f32[33,512]{1,0:T(8,128)S(1)} %convert_add_fusion.both), channel_id=1, source_target_pairs={{4,0},{8,4},{12,8},{16,12},{20,16},{24,20},{28,24},{0,28},{5,1},{9... | collective-permute-start | bytes 202760 | tf_op jit(solution)/shard_map/ppermute | solution.py:42
  9.8 2.0 %collective-permute-start.3 = (bf16[32,1024]{1,0:T(8,128)(2,1)S(1)}, bf16[32,1024]{1,0:T(8,128)(2,1)S(1)}, u32[]{:S(2)}, u32[]{:S(2)}) collective-permute-start(bf16[32,1024]{1,0:T(8,128)(2,1)S(1)} %get-tuple-element.41.own), channel_id=1, source_target_pairs={{0,1},{1,0},{2,3},{3,2},{4,5},{5,4},{6,7},{7,6},{8,9},{9,8},{10,11... | collective-permute-start | bytes 196616 | tf_op jit(solution)/shard_map/ppermute | solution.py:55
  9.8 5.5 %collective-permute-start.1 = (bf16[32,1024]{1,0:T(8,128)(2,1)S(1)}, bf16[32,1024]{1,0:T(8,128)(2,1)S(1)}, u32[]{:S(2)}, u32[]{:S(2)}) collective-permute-start(bf16[32,1024]{1,0:T(8,128)(2,1)S(1)} %get-tuple-element.41.own), channel_id=1, source_target_pairs={{0,2},{1,3},{2,0},{3,1},{4,6},{5,7},{6,4},{7,5},{8,10},{9,11},{10,... | collective-permute-start | bytes 196616 | tf_op jit(solution)/shard_map/ppermute | solution.py:55
  11.4 4.1 %collective-permute-start.2 = (bf16[32,1024]{1,0:T(8,128)(2,1)S(1)}, bf16[32,1024]{1,0:T(8,128)(2,1)S(1)}, u32[]{:S(2)}, u32[]{:S(2)}) collective-permute-start(bf16[32,1024]{1,0:T(8,128)(2,1)S(1)} %get-tuple-element.41.own), channel_id=1, source_target_pairs={{0,3},{1,2},{2,1},{3,0},{4,7},{5,6},{6,5},{7,4},{8,11},{9,10},{10,... | collective-permute-start | bytes 196616 | tf_op jit(solution)/shard_map/ppermute | solution.py:55
  17.1 5.2 %collective-permute-start.4 = (f32[32,512]{1,0:T(8,128)S(1)}, f32[32,512]{1,0:T(8,128)S(1)}, u32[]{:S(2)}, u32[]{:S(2)}) collective-permute-start(f32[32,512]{1,0:T(8,128)S(1)} %get-tuple-element.46), channel_id=1, source_target_pairs={{0,4},{4,0},{8,12},{12,8},{16,20},{20,16},{24,28},{28,24},{1,5},{5... | collective-permute-start | bytes 196616 | tf_op jit(solution)/shard_map/ppermute | solution.py:51
  17.3 7.4 %collective-permute-start.5 = (f32[32,512]{1,0:T(8,128)S(1)}, f32[32,512]{1,0:T(8,128)S(1)}, u32[]{:S(2)}, u32[]{:S(2)}) collective-permute-start(f32[32,512]{1,0:T(8,128)S(1)} %get-tuple-element.47), channel_id=1, source_target_pairs={{4,8},{8,4},{12,16},{16,12},{20,24},{24,20},{28,0},{0,28},{5,9},{9... | collective-permute-start | bytes 196616 | tf_op jit(solution)/shard_map/ppermute | solution.py:51
  25.1 1.9 %collective-permute-start.8 = (bf16[32,1024]{1,0:T(8,128)(2,1)S(1)}, bf16[32,1024]{1,0:T(8,128)(2,1)S(1)}, u32[]{:S(2)}, u32[]{:S(2)}) collective-permute-start(bf16[32,1024]{1,0:T(8,128)(2,1)S(1)} %get-tuple-element.48.own), channel_id=1, source_target_pairs={{0,1},{1,0},{2,3},{3,2},{4,5},{5,4},{6,7},{7,6},{8,9},{9,8},{10,11... | collective-permute-start | bytes 196616 | tf_op jit(solution)/shard_map/ppermute | solution.py:55
  25.2 5.4 %collective-permute-start.6 = (bf16[32,1024]{1,0:T(8,128)(2,1)S(1)}, bf16[32,1024]{1,0:T(8,128)(2,1)S(1)}, u32[]{:S(2)}, u32[]{:S(2)}) collective-permute-start(bf16[32,1024]{1,0:T(8,128)(2,1)S(1)} %get-tuple-element.48.own), channel_id=1, source_target_pairs={{0,2},{1,3},{2,0},{3,1},{4,6},{5,7},{6,4},{7,5},{8,10},{9,11},{10,... | collective-permute-start | bytes 196616 | tf_op jit(solution)/shard_map/ppermute | solution.py:55
  26.7 4.1 %collective-permute-start.7 = (bf16[32,1024]{1,0:T(8,128)(2,1)S(1)}, bf16[32,1024]{1,0:T(8,128)(2,1)S(1)}, u32[]{:S(2)}, u32[]{:S(2)}) collective-permute-start(bf16[32,1024]{1,0:T(8,128)(2,1)S(1)} %get-tuple-element.48.own), channel_id=1, source_target_pairs={{0,3},{1,2},{2,1},{3,0},{4,7},{5,6},{6,5},{7,4},{8,11},{9,10},{10,... | collective-permute-start | bytes 196616 | tf_op jit(solution)/shard_map/ppermute | solution.py:55
  33.2 14.0 %all-to-all-start = ((f32[32,1,1152]{2,1,0:T(1,128)}), f32[32,1,1152]{2,1,0:T(1,128)S(1)}, u32[]{:S(2)}, u32[]{:S(2)}) async-start(f32[32,1,1152]{2,1,0:T(1,128)} %get-tuple-element.53), calls=%async_computation | async-start | bytes 294912 | tf_op jit(solution)/shard_map/all_to_all | solution.py:291
  38.7 10.1 %collective-permute-start.9 = (f32[32,512]{1,0:T(8,128)S(1)}, f32[32,512]{1,0:T(8,128)S(1)}, u32[]{:S(2)}, u32[]{:S(2)}) collective-permute-start(f32[32,512]{1,0:T(8,128)S(1)} %get-tuple-element.56), channel_id=1, source_target_pairs={{0,4},{4,0},{8,12},{12,8},{16,20},{20,16},{24,28},{28,24},{1,5},{5... | collective-permute-start | bytes 196616 | tf_op jit(solution)/shard_map/ppermute | solution.py:51
  40.6 8.3 %collective-permute-start.10 = (f32[32,512]{1,0:T(8,128)S(1)}, f32[32,512]{1,0:T(8,128)S(1)}, u32[]{:S(2)}, u32[]{:S(2)}) collective-permute-start(f32[32,512]{1,0:T(8,128)S(1)} %get-tuple-element.57), channel_id=1, source_target_pairs={{4,8},{8,4},{12,16},{16,12},{20,24},{24,20},{28,0},{0,28},{5,9},{9... | collective-permute-start | bytes 196616 | tf_op jit(solution)/shard_map/ppermute | solution.py:51
  49.4 2.3 %collective-permute-start.13 = (bf16[32,1024]{1,0:T(8,128)(2,1)S(1)}, bf16[32,1024]{1,0:T(8,128)(2,1)S(1)}, u32[]{:S(2)}, u32[]{:S(2)}) collective-permute-start(bf16[32,1024]{1,0:T(8,128)(2,1)S(1)} %get-tuple-element.58.own), channel_id=1, source_target_pairs={{0,1},{1,0},{2,3},{3,2},{4,5},{5,4},{6,7},{7,6},{8,9},{9,8},{10,11... | collective-permute-start | bytes 196616 | tf_op jit(solution)/shard_map/ppermute | solution.py:55
  50.2 5.0 %collective-permute-start.11 = (bf16[32,1024]{1,0:T(8,128)(2,1)S(1)}, bf16[32,1024]{1,0:T(8,128)(2,1)S(1)}, u32[]{:S(2)}, u32[]{:S(2)}) collective-permute-start(bf16[32,1024]{1,0:T(8,128)(2,1)S(1)} %get-tuple-element.58.own), channel_id=1, source_target_pairs={{0,2},{1,3},{2,0},{3,1},{4,6},{5,7},{6,4},{7,5},{8,10},{9,11},{10,... | collective-permute-start | bytes 196616 | tf_op jit(solution)/shard_map/ppermute | solution.py:55
  50.3 4.9 %collective-permute-start.12 = (bf16[32,1024]{1,0:T(8,128)(2,1)S(1)}, bf16[32,1024]{1,0:T(8,128)(2,1)S(1)}, u32[]{:S(2)}, u32[]{:S(2)}) collective-permute-start(bf16[32,1024]{1,0:T(8,128)(2,1)S(1)} %get-tuple-element.58.own), channel_id=1, source_target_pairs={{0,3},{1,2},{2,1},{3,0},{4,7},{5,6},{6,5},{7,4},{8,11},{9,10},{10,... | collective-permute-start | bytes 196616 | tf_op jit(solution)/shard_map/ppermute | solution.py:55
  57.4 11.3 %all-to-all-start.1 = ((f32[32,8,128]{2,1,0:T(8,128)}), f32[32,8,128]{2,1,0:T(8,128)S(1)}, u32[]{:S(2)}, u32[]{:S(2)}) async-start(f32[32,8,128]{2,1,0:T(8,128)} %get-tuple-element.62), calls=%async_computation.1 | async-start | bytes 262144 | tf_op jit(solution)/shard_map/all_to_all | solution.py:291
  60.4 8.7 %collective-permute-start.14 = (f32[32,512]{1,0:T(8,128)S(1)}, f32[32,512]{1,0:T(8,128)S(1)}, u32[]{:S(2)}, u32[]{:S(2)}) collective-permute-start(f32[32,512]{1,0:T(8,128)S(1)} %get-tuple-element.67), channel_id=1, source_target_pairs={{0,4},{4,0},{8,12},{12,8},{16,20},{20,16},{24,28},{28,24},{1,5},{5... | collective-permute-start | bytes 196616 | tf_op jit(solution)/shard_map/ppermute | solution.py:51
  62.3 7.4 %collective-permute-start.15 = (f32[32,512]{1,0:T(8,128)S(1)}, f32[32,512]{1,0:T(8,128)S(1)}, u32[]{:S(2)}, u32[]{:S(2)}) collective-permute-start(f32[32,512]{1,0:T(8,128)S(1)} %get-tuple-element.68), channel_id=1, source_target_pairs={{4,8},{8,4},{12,16},{16,12},{20,24},{24,20},{28,0},{0,28},{5,9},{9... | collective-permute-start | bytes 196616 | tf_op jit(solution)/shard_map/ppermute | solution.py:51
  70.0 1.9 %collective-permute-start.18 = (bf16[32,1024]{1,0:T(8,128)(2,1)S(1)}, bf16[32,1024]{1,0:T(8,128)(2,1)S(1)}, u32[]{:S(2)}, u32[]{:S(2)}) collective-permute-start(bf16[32,1024]{1,0:T(8,128)(2,1)S(1)} %get-tuple-element.69.own), channel_id=1, source_target_pairs={{0,1},{1,0},{2,3},{3,2},{4,5},{5,4},{6,7},{7,6},{8,9},{9,8},{10,11... | collective-permute-start | bytes 196616 | tf_op jit(solution)/shard_map/ppermute | solution.py:55
  70.2 5.3 %collective-permute-start.16 = (bf16[32,1024]{1,0:T(8,128)(2,1)S(1)}, bf16[32,1024]{1,0:T(8,128)(2,1)S(1)}, u32[]{:S(2)}, u32[]{:S(2)}) collective-permute-start(bf16[32,1024]{1,0:T(8,128)(2,1)S(1)} %get-tuple-element.69.own), channel_id=1, source_target_pairs={{0,2},{1,3},{2,0},{3,1},{4,6},{5,7},{6,4},{7,5},{8,10},{9,11},{10,... | collective-permute-start | bytes 196616 | tf_op jit(solution)/shard_map/ppermute | solution.py:55
  71.6 4.1 %collective-permute-start.17 = (bf16[32,1024]{1,0:T(8,128)(2,1)S(1)}, bf16[32,1024]{1,0:T(8,128)(2,1)S(1)}, u32[]{:S(2)}, u32[]{:S(2)}) collective-permute-start(bf16[32,1024]{1,0:T(8,128)(2,1)S(1)} %get-tuple-element.69.own), channel_id=1, source_target_pairs={{0,3},{1,2},{2,1},{3,0},{4,7},{5,6},{6,5},{7,4},{8,11},{9,10},{10,... | collective-permute-start | bytes 196616 | tf_op jit(solution)/shard_map/ppermute | solution.py:55
  78.0 12.4 %all-to-all-start.2 = ((f32[32,8,128]{2,1,0:T(8,128)}), f32[32,8,128]{2,1,0:T(8,128)S(1)}, u32[]{:S(2)}, u32[]{:S(2)}) async-start(f32[32,8,128]{2,1,0:T(8,128)} %get-tuple-element.73), calls=%async_computation.2 | async-start | bytes 262144 | tf_op jit(solution)/shard_map/all_to_all | solution.py:291
  82.0 9.8 %collective-permute-start.19 = (f32[32,512]{1,0:T(8,128)S(1)}, f32[32,512]{1,0:T(8,128)S(1)}, u32[]{:S(2)}, u32[]{:S(2)}) collective-permute-start(f32[32,512]{1,0:T(8,128)S(1)} %get-tuple-element.76), channel_id=1, source_target_pairs={{28,0},{0,4},{4,8},{8,12},{12,16},{16,20},{20,24},{24,28},{29,1},{... | collective-permute-start | bytes 196616 | tf_op jit(solution)/shard_map/ppermute | solution.py:42

commit v2 on v1

--- a/solution.py
+++ b/solution.py
@@ -40,6 +40,12 @@
     devices = range(lax.axis_size("sx"))
     route = [((i - distance) % len(devices), i) for i in devices]
     return lax.ppermute(block, "sx", route)
+
+
+def traded(odd_block, even_block):
+    got_even = swapped(even_block, 0)
+    got_odd = swapped(odd_block, 1)
+    return got_even, got_odd
 
 
 def swapped(block, first):
@@ -330,19 +336,19 @@
     vectors = (f32(k, 2 * face), bf16(k, 2 * face))
     residual, rounded = call(join_kernel, vectors, both, following)
     product, even, odd_, tile = apply(rounded, precond_rows, residual, "first")
-    got_odd, got_even = swapped(odd_, 1), swapped(even, 0)
+    got_even, got_odd = traded(odd_, even)
     search, rounded = call(direction_kernel, vectors, product, got_even, got_odd, chosen)
 
     product, even, odd_, partials = apply(rounded, schur_rows, search, "both", tile)
     partials = spread(partials)
-    got_odd, got_even = swapped(odd_, 1), swapped(even, 0)
+    got_even, got_odd = traded(odd_, even)
     alpha, gamma = call(alpha_kernel, (f32(k, k), f32(k, k)), partials)
     residual, rounded = call(residual_kernel, vectors, alpha, product, got_even, got_odd, chosen, residual)
 
     inverse, moved = call(aside_kernel, (f32(k, k), f32(k, face)), gamma, alpha, search)
     product, even, odd_, partials = apply(rounded, precond_rows, residual, "one")
     partials = spread(partials)
-    got_odd, got_even = swapped(odd_, 1), swapped(even, 0)
+    got_even, got_odd = traded(odd_, even)
     beta, gnew = call(beta_kernel, (f32(k, k), f32(k, k)), partials, inverse)
     new_search, rounded = call(search_kernel, vectors, beta, product, got_even, got_odd, chosen, search)
 

time: 93.5 us -> 93.5 us (level)
  no operation moved by 1% of the time
where the time goes in v2:
time: 93.5 us; the launch traced here: 93 us
  starting transfers between devices  43.8 us (47%)
  Pallas kernels  30.2 us (32%)
  waiting for transfers between devices  17.3 us (19%)
    pallas_call x18, Pallas kernels, call(): pl.pallas_call(body, out_shape=outs, in_specs=places or [VMEM] * len(args...  30.2 us
    ppermute x6, starting transfers between devices, swapped(): return lax.ppermute(block, 'sx', route)  15.5 us
    all_to_all x3, starting transfers between devices, spread(): return lax.all_to_all(partials, AXES, 0, 0)  12.5 us
    all_to_all x3, waiting for transfers between devices, spread(): return lax.all_to_all(partials, AXES, 0, 0)  11.7 us
    ppermute x12, starting transfers between devices, partner(): lax.ppermute(block, 'sy', [(i, i ^ distance) for i in range(lax.axis_size...  7.98 us
    ppermute x2, starting transfers between devices, passed_along(): return lax.ppermute(block, 'sx', route)  7.85 us
    ppermute x6, waiting for transfers between devices, swapped(): return lax.ppermute(block, 'sx', route)  3.09 us
    ppermute x2, waiting for transfers between devices, passed_along(): return lax.ppermute(block, 'sx', route)  2.06 us
  transfers between devices with their start and end apart: 23, of which 9 were waited for; matrix products, arithmetic and copies ran while one was open for 0% of the time, Pallas kernels for 20%

profile of v2, /device:TPU:0, one launch (start us, length us, event | category | flops | bytes accessed | tf_op | source)
XLA Modules:
  0.0 93.0 jit_solution(17555264353950481512)
XLA Ops:
  1.5 6.0 %collective-permute-start = (f32[33,512]{1,0:T(8,128)S(1)}, f32[33,512]{1,0:T(8,128)S(1)}, u32[]{:S(2)}, u32[]{:S(2)}) collective-permute-start(f32[33,512]{1,0:T(8,128)S(1)} %convert_add_fusion.both), channel_id=1, source_target_pairs={{4,0},{8,4},{12,8},{16,12},{20,16},{24,20},{28,24},{0,28},{5,1},{9... | collective-permute-start | bytes 202760 | tf_op jit(solution)/shard_map/ppermute | solution.py:42
  7.5 2.1 %collective-permute-done.following = f32[33,512]{1,0:T(8,128)S(1)} collective-permute-done((f32[33,512]{1,0:T(8,128)S(1)}, f32[33,512]{1,0:T(8,128)S(1)}, u32[]{:S(2)}, u32[]{:S(2)}) %collective-permute-start) | collective-permute-done | bytes 67616 | tf_op jit(solution)/shard_map/ppermute | solution.py:42
  11.8 3.5 %shard_map.60 = (f32[32,1024]{1,0:T(8,128)S(1)}, bf16[2,1024,1024]{2,1,0:T(8,128)(2,1)S(1)}) custom-call(bf16[32,1024]{1,0:T(8,128)(2,1)S(1)} %get-tuple-element.41.own, bf16[32,1024]{1,0:T(8,128)(2,1)S(1)} %collective-permute-done.3.beside, bf16[1024,4096]{1,0:T(8,128)(2,1)} %bitcast.5), custom_call_target="tpu_custom_call" | custom-call | flops 16777216 | bytes 8388608 | tf_op jit(solution)/shard_map/pallas_call | solution.py:20
  15.5 1.6 %shard_map.62 = (f32[32,1024]{1,0:T(8,128)S(1)}, f32[32,512]{1,0:T(8,128)S(1)}, f32[32,512]{1,0:T(8,128)S(1)}, f32[32,32]{1,0:T(8,128)S(1)}) custom-call(bf16[32,1024]{1,0:T(8,128)(2,1)S(1)} %collective-permute-done.1.refs_0_, bf16[32,1024]{1,0:T(8,128)(2,1)S(1)} %collective-permute-done.2.refs_1_, bf16[2,1024,1024]{2,1,0:T(8,128)(2,1)S(1)} %get-tuple-element.42.refs_2_, ...), custom_call_target="tpu_custom_call" | custom-call | flops 16777216 | bytes 8388608 | tf_op jit(solution)/shard_map/pallas_call | solution.py:20
  17.3 4.9 %collective-permute-start.5 = (f32[32,512]{1,0:T(8,128)S(1)}, f32[32,512]{1,0:T(8,128)S(1)}, u32[]{:S(2)}, u32[]{:S(2)}) collective-permute-start(f32[32,512]{1,0:T(8,128)S(1)} %get-tuple-element.47), channel_id=1, source_target_pairs={{4,8},{8,4},{12,16},{16,12},{20,24},{24,20},{28,0},{0,28},{5,9},{9... | collective-permute-start | bytes 196616 | tf_op jit(solution)/shard_map/ppermute | solution.py:57
  22.3 2.5 %collective-permute-done.5.got_odd = f32[32,512]{1,0:T(8,128)S(1)} collective-permute-done((f32[32,512]{1,0:T(8,128)S(1)}, f32[32,512]{1,0:T(8,128)S(1)}, u32[]{:S(2)}, u32[]{:S(2)}) %collective-permute-start.5) | collective-permute-done | bytes 65568 | tf_op jit(solution)/shard_map/ppermute | solution.py:57
  27.0 3.5 %shard_map.64 = (f32[32,1024]{1,0:T(8,128)S(1)}, bf16[2,1024,1024]{2,1,0:T(8,128)(2,1)S(1)}) custom-call(bf16[32,1024]{1,0:T(8,128)(2,1)S(1)} %get-tuple-element.48.own, bf16[32,1024]{1,0:T(8,128)(2,1)S(1)} %collective-permute-done.8.beside, bf16[1024,4096]{1,0:T(8,128)(2,1)} %bitcast.7), custom_call_target="tpu_custom_call" | custom-call | flops 16777216 | bytes 8388608 | tf_op jit(solution)/shard_map/pallas_call | solution.py:20
  30.8 2.4 %shard_map.65 = (f32[32,1024]{1,0:T(8,128)S(1)}, f32[32,512]{1,0:T(8,128)S(1)}, f32[32,512]{1,0:T(8,128)S(1)}, f32[32,1,1152]{2,1,0:T(1,128)}) custom-call(bf16[32,1024]{1,0:T(8,128)(2,1)S(1)} %collective-permute-done.6.refs_0_, bf16[32,1024]{1,0:T(8,128)(2,1)S(1)} %collective-permute-done.7.refs_1_, bf16[2,1024,1024]{2,1,0:T(8,128)(2,1)S(1)} %get-tuple-element.49.refs_2_, ...), custom_call_target="tpu_custom_call" | custom-call | flops 16777216 | bytes 8388608 | tf_op jit(solution)/shard_map/pallas_call | solution.py:20
  33.2 5.5 %all-to-all-start = ((f32[32,1,1152]{2,1,0:T(1,128)}), f32[32,1,1152]{2,1,0:T(1,128)S(1)}, u32[]{:S(2)}, u32[]{:S(2)}) async-start(f32[32,1,1152]{2,1,0:T(1,128)} %get-tuple-element.53), calls=%async_computation | async-start | bytes 294912 | tf_op jit(solution)/shard_map/all_to_all | solution.py:297
  38.7 1.8 %collective-permute-start.9 = (f32[32,512]{1,0:T(8,128)S(1)}, f32[32,512]{1,0:T(8,128)S(1)}, u32[]{:S(2)}, u32[]{:S(2)}) collective-permute-start(f32[32,512]{1,0:T(8,128)S(1)} %get-tuple-element.56), channel_id=1, source_target_pairs={{0,4},{4,0},{8,12},{12,8},{16,20},{20,16},{24,28},{28,24},{1,5},{5... | collective-permute-start | bytes 196616 | tf_op jit(solution)/shard_map/ppermute | solution.py:57
  40.6 3.3 %collective-permute-start.10 = (f32[32,512]{1,0:T(8,128)S(1)}, f32[32,512]{1,0:T(8,128)S(1)}, u32[]{:S(2)}, u32[]{:S(2)}) collective-permute-start(f32[32,512]{1,0:T(8,128)S(1)} %get-tuple-element.57), channel_id=1, source_target_pairs={{4,8},{8,4},{12,16},{16,12},{20,24},{24,20},{28,0},{0,28},{5,9},{9... | collective-permute-start | bytes 196616 | tf_op jit(solution)/shard_map/ppermute | solution.py:57
  43.9 3.3 %all-to-all-done.partials = f32[32,1,1152]{2,1,0:T(1,128)S(1)} async-done(((f32[32,1,1152]{2,1,0:T(1,128)}), f32[32,1,1152]{2,1,0:T(1,128)S(1)}, u32[]{:S(2)}, u32[]{:S(2)}) %all-to-all-start) | async-done | bytes 147488 | tf_op jit(solution)/shard_map/all_to_all | solution.py:297
  47.2 1.6 %shard_map.66 = (f32[32,32]{1,0:T(8,128)S(1)}, f32[32,32]{1,0:T(8,128)S(1)}) custom-call(f32[32,1,1152]{2,1,0:T(1,128)S(1)} %all-to-all-done.partials), custom_call_target="tpu_custom_call" | custom-call | flops 16777216 | bytes 8388608 | tf_op jit(solution)/shard_map/pallas_call | solution.py:20
  51.6 3.5 %shard_map.68 = (f32[32,1024]{1,0:T(8,128)S(1)}, bf16[2,1024,1024]{2,1,0:T(8,128)(2,1)S(1)}) custom-call(bf16[32,1024]{1,0:T(8,128)(2,1)S(1)} %get-tuple-element.58.own, bf16[32,1024]{1,0:T(8,128)(2,1)S(1)} %collective-permute-done.13.beside, bf16[1024,4096]{1,0:T(8,128)(2,1)} %bitcast.6), custom_call_target="tpu_custom_call" | custom-call | flops 16777216 | bytes 8388608 | tf_op jit(solution)/shard_map/pallas_call | solution.py:20
  55.2 2.3 %shard_map.69 = (f32[32,1024]{1,0:T(8,128)S(1)}, f32[32,512]{1,0:T(8,128)S(1)}, f32[32,512]{1,0:T(8,128)S(1)}, f32[32,8,128]{2,1,0:T(8,128)}) custom-call(bf16[32,1024]{1,0:T(8,128)(2,1)S(1)} %collective-permute-done.11.refs_0_, bf16[32,1024]{1,0:T(8,128)(2,1)S(1)} %collective-permute-done.12.refs_1_, bf16[2,1024,1024]{2,1,0:T(8,128)(2,1)S(1)} %get-tuple-element.59.refs_2_, ...), custom_call_target="tpu_custom_call" | custom-call | flops 16777216 | bytes 8388608 | tf_op jit(solution)/shard_map/pallas_call | solution.py:20
  57.4 3.0 %all-to-all-start.1 = ((f32[32,8,128]{2,1,0:T(8,128)}), f32[32,8,128]{2,1,0:T(8,128)S(1)}, u32[]{:S(2)}, u32[]{:S(2)}) async-start(f32[32,8,128]{2,1,0:T(8,128)} %get-tuple-element.62), calls=%async_computation.1 | async-start | bytes 262144 | tf_op jit(solution)/shard_map/all_to_all | solution.py:297
  60.4 1.8 %collective-permute-start.14 = (f32[32,512]{1,0:T(8,128)S(1)}, f32[32,512]{1,0:T(8,128)S(1)}, u32[]{:S(2)}, u32[]{:S(2)}) collective-permute-start(f32[32,512]{1,0:T(8,128)S(1)} %get-tuple-element.67), channel_id=1, source_target_pairs={{0,4},{4,0},{8,12},{12,8},{16,20},{20,16},{24,28},{28,24},{1,5},{5... | collective-permute-start | bytes 196616 | tf_op jit(solution)/shard_map/ppermute | solution.py:57
  62.3 3.3 %collective-permute-start.15 = (f32[32,512]{1,0:T(8,128)S(1)}, f32[32,512]{1,0:T(8,128)S(1)}, u32[]{:S(2)}, u32[]{:S(2)}) collective-permute-start(f32[32,512]{1,0:T(8,128)S(1)} %get-tuple-element.68), channel_id=1, source_target_pairs={{4,8},{8,4},{12,16},{16,12},{20,24},{24,20},{28,0},{0,28},{5,9},{9... | collective-permute-start | bytes 196616 | tf_op jit(solution)/shard_map/ppermute | solution.py:57
  67.0 1.8 %all-to-all-done.1.partials = f32[32,8,128]{2,1,0:T(8,128)S(1)} async-done(((f32[32,8,128]{2,1,0:T(8,128)}), f32[32,8,128]{2,1,0:T(8,128)S(1)}, u32[]{:S(2)}, u32[]{:S(2)}) %all-to-all-start.1) | async-done | bytes 131104 | tf_op jit(solution)/shard_map/all_to_all | solution.py:297
  72.0 3.5 %shard_map.73 = (f32[32,1024]{1,0:T(8,128)S(1)}, bf16[2,1024,1024]{2,1,0:T(8,128)(2,1)S(1)}) custom-call(bf16[32,1024]{1,0:T(8,128)(2,1)S(1)} %get-tuple-element.69.own, bf16[32,1024]{1,0:T(8,128)(2,1)S(1)} %collective-permute-done.18.beside, bf16[1024,4096]{1,0:T(8,128)(2,1)} %bitcast.8), custom_call_target="tpu_custom_call" | custom-call | flops 16777216 | bytes 8388608 | tf_op jit(solution)/shard_map/pallas_call | solution.py:20
  75.7 2.3 %shard_map.74 = (f32[32,1024]{1,0:T(8,128)S(1)}, f32[32,512]{1,0:T(8,128)S(1)}, f32[32,8,128]{2,1,0:T(8,128)}) custom-call(bf16[32,1024]{1,0:T(8,128)(2,1)S(1)} %collective-permute-done.16.refs_0_, bf16[32,1024]{1,0:T(8,128)(2,1)S(1)} %collective-permute-done.17.refs_1_, bf16[2,1024,1024]{2,1,0:T(8,128)(2,1)S(1)} %get-tuple-element.70.refs_2_, ...), custom_call_target="tpu_custom_call" | custom-call | flops 16777216 | bytes 8388608 | tf_op jit(solution)/shard_map/pallas_call | solution.py:20
  78.0 4.0 %all-to-all-start.2 = ((f32[32,8,128]{2,1,0:T(8,128)}), f32[32,8,128]{2,1,0:T(8,128)S(1)}, u32[]{:S(2)}, u32[]{:S(2)}) async-start(f32[32,8,128]{2,1,0:T(8,128)} %get-tuple-element.73), calls=%async_computation.2 | async-start | bytes 262144 | tf_op jit(solution)/shard_map/all_to_all | solution.py:297
  82.0 1.8 %collective-permute-start.19 = (f32[32,512]{1,0:T(8,128)S(1)}, f32[32,512]{1,0:T(8,128)S(1)}, u32[]{:S(2)}, u32[]{:S(2)}) collective-permute-start(f32[32,512]{1,0:T(8,128)S(1)} %get-tuple-element.76), channel_id=1, source_target_pairs={{28,0},{0,4},{4,8},{8,12},{12,16},{16,20},{20,24},{24,28},{29,1},{... | collective-permute-start | bytes 196616 | tf_op jit(solution)/shard_map/ppermute | solution.py:42
  83.8 6.5 %all-to-all-done.2.partials = f32[32,8,128]{2,1,0:T(8,128)S(1)} async-done(((f32[32,8,128]{2,1,0:T(8,128)}), f32[32,8,128]{2,1,0:T(8,128)S(1)}, u32[]{:S(2)}, u32[]{:S(2)}) %all-to-all-start.2) | async-done | bytes 131104 | tf_op jit(solution)/shard_map/all_to_all | solution.py:297
  (41 shorter events, 16.1 us)
Async XLA Ops:
  1.5 8.1 %collective-permute-start = (f32[33,512]{1,0:T(8,128)S(1)}, f32[33,512]{1,0:T(8,128)S(1)}, u32[]{:S(2)}, u32[]{:S(2)}) collective-permute-start(f32[33,512]{1,0:T(8,128)S(1)} %convert_add_fusion.both), channel_id=1, source_target_pairs={{4,0},{8,4},{12,8},{16,12},{20,16},{24,20},{28,24},{0,28},{5,1},{9... | collective-permute-start | bytes 202760 | tf_op jit(solution)/shard_map/ppermute | solution.py:42
  9.8 2.0 %collective-permute-start.3 = (bf16[32,1024]{1,0:T(8,128)(2,1)S(1)}, bf16[32,1024]{1,0:T(8,128)(2,1)S(1)}, u32[]{:S(2)}, u32[]{:S(2)}) collective-permute-start(bf16[32,1024]{1,0:T(8,128)(2,1)S(1)} %get-tuple-element.41.own), channel_id=1, source_target_pairs={{0,1},{1,0},{2,3},{3,2},{4,5},{5,4},{6,7},{7,6},{8,9},{9,8},{10,11... | collective-permute-start | bytes 196616 | tf_op jit(solution)/shard_map/ppermute | solution.py:61
  9.8 5.5 %collective-permute-start.1 = (bf16[32,1024]{1,0:T(8,128)(2,1)S(1)}, bf16[32,1024]{1,0:T(8,128)(2,1)S(1)}, u32[]{:S(2)}, u32[]{:S(2)}) collective-permute-start(bf16[32,1024]{1,0:T(8,128)(2,1)S(1)} %get-tuple-element.41.own), channel_id=1, source_target_pairs={{0,2},{1,3},{2,0},{3,1},{4,6},{5,7},{6,4},{7,5},{8,10},{9,11},{10,... | collective-permute-start | bytes 196616 | tf_op jit(solution)/shard_map/ppermute | solution.py:61
  11.4 4.1 %collective-permute-start.2 = (bf16[32,1024]{1,0:T(8,128)(2,1)S(1)}, bf16[32,1024]{1,0:T(8,128)(2,1)S(1)}, u32[]{:S(2)}, u32[]{:S(2)}) collective-permute-start(bf16[32,1024]{1,0:T(8,128)(2,1)S(1)} %get-tuple-element.41.own), channel_id=1, source_target_pairs={{0,3},{1,2},{2,1},{3,0},{4,7},{5,6},{6,5},{7,4},{8,11},{9,10},{10,... | collective-permute-start | bytes 196616 | tf_op jit(solution)/shard_map/ppermute | solution.py:61
  17.1 5.2 %collective-permute-start.4 = (f32[32,512]{1,0:T(8,128)S(1)}, f32[32,512]{1,0:T(8,128)S(1)}, u32[]{:S(2)}, u32[]{:S(2)}) collective-permute-start(f32[32,512]{1,0:T(8,128)S(1)} %get-tuple-element.46), channel_id=1, source_target_pairs={{0,4},{4,0},{8,12},{12,8},{16,20},{20,16},{24,28},{28,24},{1,5},{5... | collective-permute-start | bytes 196616 | tf_op jit(solution)/shard_map/ppermute | solution.py:57
  17.3 7.4 %collective-permute-start.5 = (f32[32,512]{1,0:T(8,128)S(1)}, f32[32,512]{1,0:T(8,128)S(1)}, u32[]{:S(2)}, u32[]{:S(2)}) collective-permute-start(f32[32,512]{1,0:T(8,128)S(1)} %get-tuple-element.47), channel_id=1, source_target_pairs={{4,8},{8,4},{12,16},{16,12},{20,24},{24,20},{28,0},{0,28},{5,9},{9... | collective-permute-start | bytes 196616 | tf_op jit(solution)/shard_map/ppermute | solution.py:57
  25.1 1.9 %collective-permute-start.8 = (bf16[32,1024]{1,0:T(8,128)(2,1)S(1)}, bf16[32,1024]{1,0:T(8,128)(2,1)S(1)}, u32[]{:S(2)}, u32[]{:S(2)}) collective-permute-start(bf16[32,1024]{1,0:T(8,128)(2,1)S(1)} %get-tuple-element.48.own), channel_id=1, source_target_pairs={{0,1},{1,0},{2,3},{3,2},{4,5},{5,4},{6,7},{7,6},{8,9},{9,8},{10,11... | collective-permute-start | bytes 196616 | tf_op jit(solution)/shard_map/ppermute | solution.py:61
  25.2 5.4 %collective-permute-start.6 = (bf16[32,1024]{1,0:T(8,128)(2,1)S(1)}, bf16[32,1024]{1,0:T(8,128)(2,1)S(1)}, u32[]{:S(2)}, u32[]{:S(2)}) collective-permute-start(bf16[32,1024]{1,0:T(8,128)(2,1)S(1)} %get-tuple-element.48.own), channel_id=1, source_target_pairs={{0,2},{1,3},{2,0},{3,1},{4,6},{5,7},{6,4},{7,5},{8,10},{9,11},{10,... | collective-permute-start | bytes 196616 | tf_op jit(solution)/shard_map/ppermute | solution.py:61
  26.7 4.1 %collective-permute-start.7 = (bf16[32,1024]{1,0:T(8,128)(2,1)S(1)}, bf16[32,1024]{1,0:T(8,128)(2,1)S(1)}, u32[]{:S(2)}, u32[]{:S(2)}) collective-permute-start(bf16[32,1024]{1,0:T(8,128)(2,1)S(1)} %get-tuple-element.48.own), channel_id=1, source_target_pairs={{0,3},{1,2},{2,1},{3,0},{4,7},{5,6},{6,5},{7,4},{8,11},{9,10},{10,... | collective-permute-start | bytes 196616 | tf_op jit(solution)/shard_map/ppermute | solution.py:61
  33.2 14.0 %all-to-all-start = ((f32[32,1,1152]{2,1,0:T(1,128)}), f32[32,1,1152]{2,1,0:T(1,128)S(1)}, u32[]{:S(2)}, u32[]{:S(2)}) async-start(f32[32,1,1152]{2,1,0:T(1,128)} %get-tuple-element.53), calls=%async_computation | async-start | bytes 294912 | tf_op jit(solution)/shard_map/all_to_all | solution.py:297
  38.7 10.1 %collective-permute-start.9 = (f32[32,512]{1,0:T(8,128)S(1)}, f32[32,512]{1,0:T(8,128)S(1)}, u32[]{:S(2)}, u32[]{:S(2)}) collective-permute-start(f32[32,512]{1,0:T(8,128)S(1)} %get-tuple-element.56), channel_id=1, source_target_pairs={{0,4},{4,0},{8,12},{12,8},{16,20},{20,16},{24,28},{28,24},{1,5},{5... | collective-permute-start | bytes 196616 | tf_op jit(solution)/shard_map/ppermute | solution.py:57
  40.6 8.3 %collective-permute-start.10 = (f32[32,512]{1,0:T(8,128)S(1)}, f32[32,512]{1,0:T(8,128)S(1)}, u32[]{:S(2)}, u32[]{:S(2)}) collective-permute-start(f32[32,512]{1,0:T(8,128)S(1)} %get-tuple-element.57), channel_id=1, source_target_pairs={{4,8},{8,4},{12,16},{16,12},{20,24},{24,20},{28,0},{0,28},{5,9},{9... | collective-permute-start | bytes 196616 | tf_op jit(solution)/shard_map/ppermute | solution.py:57
  49.4 2.3 %collective-permute-start.13 = (bf16[32,1024]{1,0:T(8,128)(2,1)S(1)}, bf16[32,1024]{1,0:T(8,128)(2,1)S(1)}, u32[]{:S(2)}, u32[]{:S(2)}) collective-permute-start(bf16[32,1024]{1,0:T(8,128)(2,1)S(1)} %get-tuple-element.58.own), channel_id=1, source_target_pairs={{0,1},{1,0},{2,3},{3,2},{4,5},{5,4},{6,7},{7,6},{8,9},{9,8},{10,11... | collective-permute-start | bytes 196616 | tf_op jit(solution)/shard_map/ppermute | solution.py:61
  50.2 5.0 %collective-permute-start.11 = (bf16[32,1024]{1,0:T(8,128)(2,1)S(1)}, bf16[32,1024]{1,0:T(8,128)(2,1)S(1)}, u32[]{:S(2)}, u32[]{:S(2)}) collective-permute-start(bf16[32,1024]{1,0:T(8,128)(2,1)S(1)} %get-tuple-element.58.own), channel_id=1, source_target_pairs={{0,2},{1,3},{2,0},{3,1},{4,6},{5,7},{6,4},{7,5},{8,10},{9,11},{10,... | collective-permute-start | bytes 196616 | tf_op jit(solution)/shard_map/ppermute | solution.py:61
  50.3 4.9 %collective-permute-start.12 = (bf16[32,1024]{1,0:T(8,128)(2,1)S(1)}, bf16[32,1024]{1,0:T(8,128)(2,1)S(1)}, u32[]{:S(2)}, u32[]{:S(2)}) collective-permute-start(bf16[32,1024]{1,0:T(8,128)(2,1)S(1)} %get-tuple-element.58.own), channel_id=1, source_target_pairs={{0,3},{1,2},{2,1},{3,0},{4,7},{5,6},{6,5},{7,4},{8,11},{9,10},{10,... | collective-permute-start | bytes 196616 | tf_op jit(solution)/shard_map/ppermute | solution.py:61
  57.4 11.3 %all-to-all-start.1 = ((f32[32,8,128]{2,1,0:T(8,128)}), f32[32,8,128]{2,1,0:T(8,128)S(1)}, u32[]{:S(2)}, u32[]{:S(2)}) async-start(f32[32,8,128]{2,1,0:T(8,128)} %get-tuple-element.62), calls=%async_computation.1 | async-start | bytes 262144 | tf_op jit(solution)/shard_map/all_to_all | solution.py:297
  60.4 8.7 %collective-permute-start.14 = (f32[32,512]{1,0:T(8,128)S(1)}, f32[32,512]{1,0:T(8,128)S(1)}, u32[]{:S(2)}, u32[]{:S(2)}) collective-permute-start(f32[32,512]{1,0:T(8,128)S(1)} %get-tuple-element.67), channel_id=1, source_target_pairs={{0,4},{4,0},{8,12},{12,8},{16,20},{20,16},{24,28},{28,24},{1,5},{5... | collective-permute-start | bytes 196616 | tf_op jit(solution)/shard_map/ppermute | solution.py:57
  62.3 7.4 %collective-permute-start.15 = (f32[32,512]{1,0:T(8,128)S(1)}, f32[32,512]{1,0:T(8,128)S(1)}, u32[]{:S(2)}, u32[]{:S(2)}) collective-permute-start(f32[32,512]{1,0:T(8,128)S(1)} %get-tuple-element.68), channel_id=1, source_target_pairs={{4,8},{8,4},{12,16},{16,12},{20,24},{24,20},{28,0},{0,28},{5,9},{9... | collective-permute-start | bytes 196616 | tf_op jit(solution)/shard_map/ppermute | solution.py:57
  70.0 1.9 %collective-permute-start.18 = (bf16[32,1024]{1,0:T(8,128)(2,1)S(1)}, bf16[32,1024]{1,0:T(8,128)(2,1)S(1)}, u32[]{:S(2)}, u32[]{:S(2)}) collective-permute-start(bf16[32,1024]{1,0:T(8,128)(2,1)S(1)} %get-tuple-element.69.own), channel_id=1, source_target_pairs={{0,1},{1,0},{2,3},{3,2},{4,5},{5,4},{6,7},{7,6},{8,9},{9,8},{10,11... | collective-permute-start | bytes 196616 | tf_op jit(solution)/shard_map/ppermute | solution.py:61
  70.2 5.3 %collective-permute-start.16 = (bf16[32,1024]{1,0:T(8,128)(2,1)S(1)}, bf16[32,1024]{1,0:T(8,128)(2,1)S(1)}, u32[]{:S(2)}, u32[]{:S(2)}) collective-permute-start(bf16[32,1024]{1,0:T(8,128)(2,1)S(1)} %get-tuple-element.69.own), channel_id=1, source_target_pairs={{0,2},{1,3},{2,0},{3,1},{4,6},{5,7},{6,4},{7,5},{8,10},{9,11},{10,... | collective-permute-start | bytes 196616 | tf_op jit(solution)/shard_map/ppermute | solution.py:61
  71.6 4.1 %collective-permute-start.17 = (bf16[32,1024]{1,0:T(8,128)(2,1)S(1)}, bf16[32,1024]{1,0:T(8,128)(2,1)S(1)}, u32[]{:S(2)}, u32[]{:S(2)}) collective-permute-start(bf16[32,1024]{1,0:T(8,128)(2,1)S(1)} %get-tuple-element.69.own), channel_id=1, source_target_pairs={{0,3},{1,2},{2,1},{3,0},{4,7},{5,6},{6,5},{7,4},{8,11},{9,10},{10,... | collective-permute-start | bytes 196616 | tf_op jit(solution)/shard_map/ppermute | solution.py:61
  78.0 12.4 %all-to-all-start.2 = ((f32[32,8,128]{2,1,0:T(8,128)}), f32[32,8,128]{2,1,0:T(8,128)S(1)}, u32[]{:S(2)}, u32[]{:S(2)}) async-start(f32[32,8,128]{2,1,0:T(8,128)} %get-tuple-element.73), calls=%async_computation.2 | async-start | bytes 262144 | tf_op jit(solution)/shard_map/all_to_all | solution.py:297
  82.0 9.8 %collective-permute-start.19 = (f32[32,512]{1,0:T(8,128)S(1)}, f32[32,512]{1,0:T(8,128)S(1)}, u32[]{:S(2)}, u32[]{:S(2)}) collective-permute-start(f32[32,512]{1,0:T(8,128)S(1)} %get-tuple-element.76), channel_id=1, source_target_pairs={{28,0},{0,4},{4,8},{8,12},{12,16},{16,20},{20,24},{24,28},{29,1},{... | collective-permute-start | bytes 196616 | tf_op jit(solution)/shard_map/ppermute | solution.py:42
